TPU v7x, 128 devices: a whole 4x4x4 slice. The times are simulated.
128 devices in a mesh: blk: 8 (over z_lo, y), inner: 16 (over x, z_hi, core).
Axes of the slice: x: 4, y: 4, z: 4 (z_hi: 2, z_lo: 2; z = z_hi * 2 + z_lo), core: 2. Of those that a mesh axis runs over, the one named last changes fastest.
Arguments:
- queries: bfloat16 [16384, 768], P(('blk', 'inner')), may hold values from -16 to 16
- keys: bfloat16 [16384, 768], P(('blk', 'inner')), may hold values from -16 to 16
- values: bfloat16 [16384, 768], P(('blk', 'inner')), may hold values from -6 to 6
- valid: int32 [16384], P(('blk', 'inner')), may hold values 0 or 1
- out_weight: bfloat16 [768, 768], replicated, may hold values from -0.21875 to 0.21875
Outputs:
- mixed: bfloat16 [16384, 768], P(('blk', 'inner'))
All inputs are finite; a program needn't handle non-finite values. No bound on the sum of `valid` on one device may be relied on, other than what follows from the above.
Results may differ from a plain program's by a relative error of at most 0.015.
Values may be sent and summed in bfloat16 or wider, within the bound.
A program may use at most 128 MiB of HBM per device.

v0:
```python
import jax
import jax.numpy as jnp
from jax import lax
from jax.sharding import PartitionSpec as P

HEADS = 12
HEAD_DIM = 64


def make_fold(query_all):
    query_count = query_all.shape[0]
    query_heads = query_all.reshape(query_count, HEADS, HEAD_DIM)
    score_scale = HEAD_DIM ** (-0.5)

    def attend(state_now, piece, start):
        key_piece, value_piece, flag_piece = piece
        piece_rows = key_piece.shape[0]
        block_rows = 128
        count = piece_rows // block_rows
        key_blocks = key_piece.reshape(count, block_rows, HEADS, HEAD_DIM)
        value_blocks = value_piece.reshape(count, block_rows, HEADS, HEAD_DIM)
        flag_blocks = flag_piece.reshape(count, block_rows)

        def one_block(carry, item):
            run_max, row_total, weighted = carry
            key_heads, value_heads, flag_block = item
            scores = (
                jnp.einsum(
                    "qhd,khd->hqk", query_heads, key_heads, preferred_element_type=jnp.float32
                )
                * score_scale
            )
            scores = jnp.where(flag_block[None, None, :] > 0, scores, -1e30)
            new_max = jnp.maximum(run_max, jnp.max(scores, axis=-1))
            shrink = jnp.exp(run_max - new_max)
            chances = jnp.exp(scores - new_max[..., None]).astype(jnp.bfloat16)
            row_total = row_total * shrink + jnp.sum(chances, axis=-1, dtype=jnp.float32)
            weighted = weighted * shrink[..., None] + jnp.einsum(
                "hqk,khd->hqd", chances, value_heads, preferred_element_type=jnp.float32
            )
            return ((new_max, row_total, weighted), None)

        state_end, unused = lax.scan(one_block, state_now, (key_blocks, value_blocks, flag_blocks))
        return state_end

    starting = (
        jnp.zeros((HEADS, query_count), jnp.float32),
        jnp.zeros((HEADS, query_count), jnp.float32),
        jnp.zeros((HEADS, query_count, HEAD_DIM), jnp.float32),
    )
    return (attend, starting)


def settle(top, row_total, weighted):
    return weighted / (jnp.exp(-top) + row_total)[..., None]


def combine_loop(state_end, own_rows):
    run_max, row_total, weighted = state_end
    top = lax.pmax(run_max, "blk")
    shrink = jnp.exp(run_max - top)
    total_own, weighted_own = (
        lax.psum_scatter(row_total * shrink, "blk", scatter_dimension=1, tiled=True),
        lax.psum_scatter(weighted * shrink[..., None], "blk", scatter_dimension=1, tiled=True),
    )
    top_own = lax.dynamic_slice_in_dim(top, lax.axis_index("blk") * own_rows, own_rows, 1)
    return settle(top_own, total_own, weighted_own)


def on_device(queries, keys, values, valid, out_weight):
    own_rows = queries.shape[0]
    width = queries.shape[1]
    flags = valid.astype(jnp.bfloat16)
    query_all = lax.all_gather(queries, "blk", axis=0, tiled=True)
    attend, starting = make_fold(query_all)
    state_end = attend(
        starting,
        (
            lax.all_gather(keys, "inner", axis=0, tiled=True),
            lax.all_gather(values, "inner", axis=0, tiled=True),
            lax.all_gather(flags, "inner", axis=0, tiled=True),
        ),
        jnp.int32(0),
    )
    attended = combine_loop(state_end, own_rows)
    attended = jnp.transpose(attended, (1, 0, 2)).reshape(own_rows, width).astype(jnp.bfloat16)
    return jnp.dot(attended, out_weight, preferred_element_type=jnp.float32).astype(jnp.bfloat16)


def solution(mesh):
    return jax.shard_map(
        on_device,
        mesh=mesh,
        in_specs=(
            P(("blk", "inner"), None),
            P(("blk", "inner"), None),
            P(("blk", "inner"), None),
            P(("blk", "inner")),
            P(),
        ),
        out_specs=P(("blk", "inner"), None),
        check_vma=False,
    )
```

profile of v0, /device:TPU:1, one launch (start us, length us, event | category | flops | bytes accessed | tf_op | source)
XLA Modules:
  0.0 529.8 jit_solution(9887534371943158650)
XLA Ops:
  9.5 26.2 %all-gather = bf16[16,1,128]{2,1,0:T(2,128)(2,1)S(1)} all-gather(bf16[1,1,128]{2,1,0:T(2,128)(2,1)S(1)} %convert_bitcast_fusion), channel_id=1, replica_groups=mesh['blk'=8,'inner'=16] {'inner'}, dimensions={0}, use_global_device_ids=true | all-gather | bytes 4352 | tf_op jit(solution)/shard_map/all_gather | solution.py:81
  35.7 12.2 %all-gather.7.cloned.1.call-done = bf16[1024,768]{1,0:T(8,128)(2,1)} async-done(((bf16[128,768]{1,0:T(8,128)(2,1)}), bf16[1024,768]{1,0:T(8,128)(2,1)}) %all-gather.7.cloned.1.call-update) | async-done | bytes 1572880 | tf_op jit(solution)/shard_map/all_gather | solution.py:74
  49.5 57.7 %all-gather.5.cloned.1.call-done = bf16[2048,768]{1,0:T(8,128)(2,1)} async-done(((bf16[128,768]{1,0:T(8,128)(2,1)}), bf16[2048,768]{1,0:T(8,128)(2,1)}) %all-gather.5.cloned.1.call-update) | async-done | bytes 3145744 | tf_op jit(solution)/shard_map/all_gather | solution.py:79
  117.4 43.1 %all-gather.9.cloned.1.call-done = bf16[2048,768]{1,0:T(8,128)(2,1)} async-done(((bf16[128,768]{1,0:T(8,128)(2,1)}), bf16[2048,768]{1,0:T(8,128)(2,1)}) %all-gather.9.cloned.1.call-update) | async-done | bytes 3145744 | tf_op jit(solution)/shard_map/all_gather | solution.py:80
  170.6 238.6 %while.15 = (s32[]{:T(128)}, f32[12,1024]{1,0:T(8,128)S(1)}, f32[12,1024]{1,0:T(8,128)S(1)}, f32[12,1024,64]{1,2,0:T(8,128)}, bf16[16,128]{1,0:T(8,128)(2,1)S(1)...) while((s32[]{:T(128)}, f32[12,1024]{1,0:T(8,128)S(1)}, ...), condition=%wide.region_3.4_spmd.clone, body=%wide.region_0.3_spmd.clone.sunk | while | flops 425521536 | bytes 53086096 | solution.py:43
  170.7 4.8 bitcast_reduce_fusion.2
  184.6 4.8 bitcast_reduce_fusion.2
  194.0 5.5 %fusion.25 = f32[12,1024,64]{1,2,0:T(8,128)} fusion(f32[12,1024,64]{1,2,0:T(8,128)} %get-tuple-element.187, f32[12,1024]{1,0:T(8,128)S(1)} %get-tuple-element.173, pred[]{:T(512)S(6)} %compare.3, bf16[16,128,12,64]{1,3,2,0:T(8,128)(2,1)} %get-tuple-element.201, s32[]{:T(128)} %get-tuple-element.184, f32[12,128,1024]{2,1,0:T(8,128)S(1)} %copy-done.1, ...), kind=kOutput, calls=%fused_computation.7.clone.1 | convolution fusion | flops 209977344 | bytes 12878465 | tf_op jit(solution)/shard_map/while/body/eval_jaxpr/hqk,khd->hqd/dot_general | solution.py:38
  209.0 5.5 %fusion.25 = f32[12,1024,64]{1,2,0:T(8,128)} fusion(f32[12,1024,64]{1,2,0:T(8,128)} %get-tuple-element.187, f32[12,1024]{1,0:T(8,128)S(1)} %get-tuple-element.173, pred[]{:T(512)S(6)} %compare.3, bf16[16,128,12,64]{1,3,2,0:T(8,128)(2,1)} %get-tuple-element.201, s32[]{:T(128)} %get-tuple-element.184, f32[12,128,1024]{2,1,0:T(8,128)S(1)} %copy-done.1, ...), kind=kOutput, calls=%fused_computation.7.clone.1 | convolution fusion | flops 209977344 | bytes 12878465 | tf_op jit(solution)/shard_map/while/body/eval_jaxpr/hqk,khd->hqd/dot_general | solution.py:38
  214.5 4.8 bitcast_reduce_fusion.2
  224.0 5.5 %fusion.25 = f32[12,1024,64]{1,2,0:T(8,128)} fusion(f32[12,1024,64]{1,2,0:T(8,128)} %get-tuple-element.187, f32[12,1024]{1,0:T(8,128)S(1)} %get-tuple-element.173, pred[]{:T(512)S(6)} %compare.3, bf16[16,128,12,64]{1,3,2,0:T(8,128)(2,1)} %get-tuple-element.201, s32[]{:T(128)} %get-tuple-element.184, f32[12,128,1024]{2,1,0:T(8,128)S(1)} %copy-done.1, ...), kind=kOutput, calls=%fused_computation.7.clone.1 | convolution fusion | flops 209977344 | bytes 12878465 | tf_op jit(solution)/shard_map/while/body/eval_jaxpr/hqk,khd->hqd/dot_general | solution.py:38
  238.9 5.5 %fusion.25 = f32[12,1024,64]{1,2,0:T(8,128)} fusion(f32[12,1024,64]{1,2,0:T(8,128)} %get-tuple-element.187, f32[12,1024]{1,0:T(8,128)S(1)} %get-tuple-element.173, pred[]{:T(512)S(6)} %compare.3, bf16[16,128,12,64]{1,3,2,0:T(8,128)(2,1)} %get-tuple-element.201, s32[]{:T(128)} %get-tuple-element.184, f32[12,128,1024]{2,1,0:T(8,128)S(1)} %copy-done.1, ...), kind=kOutput, calls=%fused_computation.7.clone.1 | convolution fusion | flops 209977344 | bytes 12878465 | tf_op jit(solution)/shard_map/while/body/eval_jaxpr/hqk,khd->hqd/dot_general | solution.py:38
  244.5 4.8 bitcast_reduce_fusion.2
  253.9 5.5 %fusion.25 = f32[12,1024,64]{1,2,0:T(8,128)} fusion(f32[12,1024,64]{1,2,0:T(8,128)} %get-tuple-element.187, f32[12,1024]{1,0:T(8,128)S(1)} %get-tuple-element.173, pred[]{:T(512)S(6)} %compare.3, bf16[16,128,12,64]{1,3,2,0:T(8,128)(2,1)} %get-tuple-element.201, s32[]{:T(128)} %get-tuple-element.184, f32[12,128,1024]{2,1,0:T(8,128)S(1)} %copy-done.1, ...), kind=kOutput, calls=%fused_computation.7.clone.1 | convolution fusion | flops 209977344 | bytes 12878465 | tf_op jit(solution)/shard_map/while/body/eval_jaxpr/hqk,khd->hqd/dot_general | solution.py:38
  268.9 5.5 %fusion.25 = f32[12,1024,64]{1,2,0:T(8,128)} fusion(f32[12,1024,64]{1,2,0:T(8,128)} %get-tuple-element.187, f32[12,1024]{1,0:T(8,128)S(1)} %get-tuple-element.173, pred[]{:T(512)S(6)} %compare.3, bf16[16,128,12,64]{1,3,2,0:T(8,128)(2,1)} %get-tuple-element.201, s32[]{:T(128)} %get-tuple-element.184, f32[12,128,1024]{2,1,0:T(8,128)S(1)} %copy-done.1, ...), kind=kOutput, calls=%fused_computation.7.clone.1 | convolution fusion | flops 209977344 | bytes 12878465 | tf_op jit(solution)/shard_map/while/body/eval_jaxpr/hqk,khd->hqd/dot_general | solution.py:38
  274.4 4.8 bitcast_reduce_fusion.2
  283.9 5.5 %fusion.25 = f32[12,1024,64]{1,2,0:T(8,128)} fusion(f32[12,1024,64]{1,2,0:T(8,128)} %get-tuple-element.187, f32[12,1024]{1,0:T(8,128)S(1)} %get-tuple-element.173, pred[]{:T(512)S(6)} %compare.3, bf16[16,128,12,64]{1,3,2,0:T(8,128)(2,1)} %get-tuple-element.201, s32[]{:T(128)} %get-tuple-element.184, f32[12,128,1024]{2,1,0:T(8,128)S(1)} %copy-done.1, ...), kind=kOutput, calls=%fused_computation.7.clone.1 | convolution fusion | flops 209977344 | bytes 12878465 | tf_op jit(solution)/shard_map/while/body/eval_jaxpr/hqk,khd->hqd/dot_general | solution.py:38
  298.9 5.5 %fusion.25 = f32[12,1024,64]{1,2,0:T(8,128)} fusion(f32[12,1024,64]{1,2,0:T(8,128)} %get-tuple-element.187, f32[12,1024]{1,0:T(8,128)S(1)} %get-tuple-element.173, pred[]{:T(512)S(6)} %compare.3, bf16[16,128,12,64]{1,3,2,0:T(8,128)(2,1)} %get-tuple-element.201, s32[]{:T(128)} %get-tuple-element.184, f32[12,128,1024]{2,1,0:T(8,128)S(1)} %copy-done.1, ...), kind=kOutput, calls=%fused_computation.7.clone.1 | convolution fusion | flops 209977344 | bytes 12878465 | tf_op jit(solution)/shard_map/while/body/eval_jaxpr/hqk,khd->hqd/dot_general | solution.py:38
  304.4 4.8 bitcast_reduce_fusion.2
  313.8 5.5 %fusion.25 = f32[12,1024,64]{1,2,0:T(8,128)} fusion(f32[12,1024,64]{1,2,0:T(8,128)} %get-tuple-element.187, f32[12,1024]{1,0:T(8,128)S(1)} %get-tuple-element.173, pred[]{:T(512)S(6)} %compare.3, bf16[16,128,12,64]{1,3,2,0:T(8,128)(2,1)} %get-tuple-element.201, s32[]{:T(128)} %get-tuple-element.184, f32[12,128,1024]{2,1,0:T(8,128)S(1)} %copy-done.1, ...), kind=kOutput, calls=%fused_computation.7.clone.1 | convolution fusion | flops 209977344 | bytes 12878465 | tf_op jit(solution)/shard_map/while/body/eval_jaxpr/hqk,khd->hqd/dot_general | solution.py:38
  328.8 5.5 %fusion.25 = f32[12,1024,64]{1,2,0:T(8,128)} fusion(f32[12,1024,64]{1,2,0:T(8,128)} %get-tuple-element.187, f32[12,1024]{1,0:T(8,128)S(1)} %get-tuple-element.173, pred[]{:T(512)S(6)} %compare.3, bf16[16,128,12,64]{1,3,2,0:T(8,128)(2,1)} %get-tuple-element.201, s32[]{:T(128)} %get-tuple-element.184, f32[12,128,1024]{2,1,0:T(8,128)S(1)} %copy-done.1, ...), kind=kOutput, calls=%fused_computation.7.clone.1 | convolution fusion | flops 209977344 | bytes 12878465 | tf_op jit(solution)/shard_map/while/body/eval_jaxpr/hqk,khd->hqd/dot_general | solution.py:38
  334.4 4.8 bitcast_reduce_fusion.2
  343.8 5.5 %fusion.25 = f32[12,1024,64]{1,2,0:T(8,128)} fusion(f32[12,1024,64]{1,2,0:T(8,128)} %get-tuple-element.187, f32[12,1024]{1,0:T(8,128)S(1)} %get-tuple-element.173, pred[]{:T(512)S(6)} %compare.3, bf16[16,128,12,64]{1,3,2,0:T(8,128)(2,1)} %get-tuple-element.201, s32[]{:T(128)} %get-tuple-element.184, f32[12,128,1024]{2,1,0:T(8,128)S(1)} %copy-done.1, ...), kind=kOutput, calls=%fused_computation.7.clone.1 | convolution fusion | flops 209977344 | bytes 12878465 | tf_op jit(solution)/shard_map/while/body/eval_jaxpr/hqk,khd->hqd/dot_general | solution.py:38
  358.8 5.5 %fusion.25 = f32[12,1024,64]{1,2,0:T(8,128)} fusion(f32[12,1024,64]{1,2,0:T(8,128)} %get-tuple-element.187, f32[12,1024]{1,0:T(8,128)S(1)} %get-tuple-element.173, pred[]{:T(512)S(6)} %compare.3, bf16[16,128,12,64]{1,3,2,0:T(8,128)(2,1)} %get-tuple-element.201, s32[]{:T(128)} %get-tuple-element.184, f32[12,128,1024]{2,1,0:T(8,128)S(1)} %copy-done.1, ...), kind=kOutput, calls=%fused_computation.7.clone.1 | convolution fusion | flops 209977344 | bytes 12878465 | tf_op jit(solution)/shard_map/while/body/eval_jaxpr/hqk,khd->hqd/dot_general | solution.py:38
  364.3 4.8 bitcast_reduce_fusion.2
  373.8 5.5 %fusion.25 = f32[12,1024,64]{1,2,0:T(8,128)} fusion(f32[12,1024,64]{1,2,0:T(8,128)} %get-tuple-element.187, f32[12,1024]{1,0:T(8,128)S(1)} %get-tuple-element.173, pred[]{:T(512)S(6)} %compare.3, bf16[16,128,12,64]{1,3,2,0:T(8,128)(2,1)} %get-tuple-element.201, s32[]{:T(128)} %get-tuple-element.184, f32[12,128,1024]{2,1,0:T(8,128)S(1)} %copy-done.1, ...), kind=kOutput, calls=%fused_computation.7.clone.1 | convolution fusion | flops 209977344 | bytes 12878465 | tf_op jit(solution)/shard_map/while/body/eval_jaxpr/hqk,khd->hqd/dot_general | solution.py:38
  388.7 5.5 %fusion.25 = f32[12,1024,64]{1,2,0:T(8,128)} fusion(f32[12,1024,64]{1,2,0:T(8,128)} %get-tuple-element.187, f32[12,1024]{1,0:T(8,128)S(1)} %get-tuple-element.173, pred[]{:T(512)S(6)} %compare.3, bf16[16,128,12,64]{1,3,2,0:T(8,128)(2,1)} %get-tuple-element.201, s32[]{:T(128)} %get-tuple-element.184, f32[12,128,1024]{2,1,0:T(8,128)S(1)} %copy-done.1, ...), kind=kOutput, calls=%fused_computation.7.clone.1 | convolution fusion | flops 209977344 | bytes 12878465 | tf_op jit(solution)/shard_map/while/body/eval_jaxpr/hqk,khd->hqd/dot_general | solution.py:38
  394.3 4.8 bitcast_reduce_fusion.2
  403.7 5.5 %fusion.25 = f32[12,1024,64]{1,2,0:T(8,128)} fusion(f32[12,1024,64]{1,2,0:T(8,128)} %get-tuple-element.187, f32[12,1024]{1,0:T(8,128)S(1)} %get-tuple-element.173, pred[]{:T(512)S(6)} %compare.3, bf16[16,128,12,64]{1,3,2,0:T(8,128)(2,1)} %get-tuple-element.201, s32[]{:T(128)} %get-tuple-element.184, f32[12,128,1024]{2,1,0:T(8,128)S(1)} %copy-done.1, ...), kind=kOutput, calls=%fused_computation.7.clone.1 | convolution fusion | flops 209977344 | bytes 12878465 | tf_op jit(solution)/shard_map/while/body/eval_jaxpr/hqk,khd->hqd/dot_general | solution.py:38
  409.3 26.7 %pmax.7 = f32[12,1024]{1,0:T(8,128)S(1)} all-reduce(f32[12,1024]{1,0:T(8,128)S(1)} %get-tuple-element.50), channel_id=1, replica_groups=mesh['blk'=8,'inner'=16] {'blk'}, use_global_device_ids=true, to_apply=%region_4.5 | all-reduce | flops 12288 | bytes 98304 | tf_op jit(solution)/shard_map/pmax | solution.py:60
  440.9 31.1 %reduce-scatter.5.cloned.1.call-done = f32[12,128]{1,0:T(8,128)} async-done(((f32[12,1024]{1,0:T(8,128)}), f32[12,128]{1,0:T(8,128)}) %reduce-scatter.5.cloned.1.call-update) | async-done | bytes 6160 | tf_op jit(solution)/shard_map/reduce_scatter | solution.py:63
  472.7 48.5 %reduce-scatter.3.cloned.1.call-done = f32[12,128,64]{1,2,0:T(8,128)} async-done(((f32[12,1024,64]{1,2,0:T(8,128)}), f32[12,128,64]{1,2,0:T(8,128)}) %reduce-scatter.3.cloned.1.call-update) | async-done | bytes 393232 | tf_op jit(solution)/shard_map/reduce_scatter | solution.py:64
  (149 shorter events, 144.4 us)
Async XLA Ops:
  6.5 515.7 %copy-start = (bf16[768,768]{1,0:T(8,128)(2,1)S(1)}, bf16[768,768]{1,0:T(8,128)(2,1)}, u32[]{:S(2)}) copy-start(bf16[768,768]{1,0:T(8,128)(2,1)} %param.11) | copy-start | bytes 3538948
  6.5 41.3 %all-gather.7.cloned.1.call-start = ((), (), s32[]{:S(2)}) async-start(), calls=%async_computation.3 | async-start | bytes 1769472 | tf_op jit(solution)/shard_map/all_gather | solution.py:74
  7.3 100.0 %all-gather.5.cloned.1.call-start = ((), (), s32[]{:S(2)}) async-start(), calls=%async_computation.2 | async-start | bytes 3342336 | tf_op jit(solution)/shard_map/all_gather | solution.py:79
  8.0 152.6 %all-gather.9.cloned.1.call-start = ((), (), s32[]{:S(2)}) async-start(), calls=%async_computation.4 | async-start | bytes 3342336 | tf_op jit(solution)/shard_map/all_gather | solution.py:80
  8.7 463.2 %reduce-scatter.5.cloned.1.call-start = ((), (), s32[]{:S(2)}) async-start(), calls=%async_computation.6 | async-start | bytes 73728 | tf_op jit(solution)/shard_map/reduce_scatter | solution.py:63
  175.5 4.6 copy-start.1
  189.4 4.6 copy-start.1
  204.4 4.6 copy-start.1
  219.3 4.6 copy-start.1
  234.3 4.6 copy-start.1
  249.3 4.6 copy-start.1
  264.3 4.6 copy-start.1
  279.3 4.6 copy-start.1
  294.3 4.6 copy-start.1
  309.2 4.6 copy-start.1
  324.2 4.6 copy-start.1
  339.2 4.6 copy-start.1
  354.2 4.6 copy-start.1
  369.2 4.6 copy-start.1
  384.1 4.6 copy-start.1
  399.1 4.6 copy-start.1
  436.7 84.5 %reduce-scatter.3.cloned.1.call-start = ((), (), s32[]{:S(2)}) async-start(), calls=%async_computation.5 | async-start | bytes 3538944 | tf_op jit(solution)/shard_map/reduce_scatter | solution.py:64
Sparse Core Ops, SparseCore 0:
  9.0 38.7 all-gather.6
  50.2 56.9 all-gather.4
  109.6 50.8 all-gather.8
  436.8 35.1 reduce-scatter.4
  474.4 46.7 reduce-scatter.2
where the time goes:
time: 534 us; the launch traced here: 530 us
  waiting for transfers between devices  195 us (37%)
  matrix products  166 us (31%)
  other arithmetic  77.2 us (14%)
  blocking collectives  52.9 us (10%)
  local copies, waits for them, and re-layouts  25.7 us (5%)
  between operations  13.2 us (2%)
    dot_general x16, matrix products, one_block(): jnp.einsum('hqk,khd->hqd', chances, value_heads, preferred_element_type=j...  87.4 us
    dot_general x16, matrix products, one_block(): jnp.einsum('qhd,khd->hqk', query_heads, key_heads, preferred_element_type...  77.1 us
    reduce_sum x16, other arithmetic, one_block(): jnp.sum(chances, axis=-1, dtype=jnp.float32)  69 us
    all_gather x1, waiting for transfers between devices, on_device(): lax.all_gather(keys, 'inner', axis=0, tiled=True)  57.7 us
    reduce_scatter x1, waiting for transfers between devices, combine_loop(): lax.psum_scatter(weighted * shrink[..., None], 'blk', scatter_dimension=1...  48.5 us
    all_gather x1, waiting for transfers between devices, on_device(): lax.all_gather(values, 'inner', axis=0, tiled=True)  43.1 us
    reduce_scatter x1, waiting for transfers between devices, combine_loop(): lax.psum_scatter(row_total * shrink, 'blk', scatter_dimension=1, tiled=True)  31.1 us
    pmax x1, blocking collectives, combine_loop(): top = lax.pmax(run_max, 'blk')  26.7 us
  transfers between devices with their start and end apart: 5, of which 5 were waited for; matrix products, arithmetic and copies ran while one was open for 3% of the time, Pallas kernels for 0%

commit v1 on v0

v1 whole, which is shorter than its diff:
```python
import jax
import jax.numpy as jnp
from jax import lax
from jax.experimental import pallas as pl
from jax.experimental.pallas import tpu as pltpu
from jax.sharding import PartitionSpec as P

HEADS = 12
HEAD_DIM = 64
GROUPS = 4
GH = HEADS // GROUPS
ROWS = 128
GD = GH * HEAD_DIM
TILE = 4 * ROWS
KROWS = 2 * ROWS
SHARD = KROWS + GD + 16
LOG2E = 1.4426950408889634
MESH = pl.DeviceIdType.MESH

KA, QA, KX, KS, QY, OY, SY, OZ = 0, 4, 8, 12, 16, 20, 24, 28


def kernel(
    kv_src, q_src, w_ref, out_ref,
    kv, qb, qs, q2, sb, acc, top, shrink, o_send, s_send, o_recv, s_recv, a_send, att,
    send_sem, recv_sem,
):
    blk = lax.axis_index("blk")
    inner = lax.axis_index("inner")
    y, x, c = blk % 4, inner // 4, inner % 2
    z = (inner // 2 % 2) * 2 + blk // 4

    def at(dx=0, dy=0, dz=0, dc=0):
        tx, ty, tz, tc = (x + dx) % 4, (y + dy) % 4, (z + dz) % 4, (c + dc) % 2
        return ((tz % 2) * 4 + ty, tx * 4 + (tz // 2) * 2 + tc)

    def send(src, dst, number, device):
        return pltpu.make_async_remote_copy(
            src_ref=src, dst_ref=dst, send_sem=send_sem.at[number], recv_sem=recv_sem.at[number],
            device_id=device, device_id_type=MESH,
        )

    def keys_z(r):
        return send(kv_src.at[(z + r) % 4], kv.at[0, 0, r], KA + r, at(dz=r))

    def queries_z(r):
        return send(q_src.at[(z + r) % 4], qb.at[0, r], QA + r, at(dz=r))

    def keys_x(r):
        return send(kv.at[0, 0], kv.at[0, r], KX + r, at(dx=r))

    def keys_core(r):
        return send(kv.at[0, r], kv.at[1, r], KS + r, at(dc=1))

    def queries_y(r):
        return send(qb.at[0], qb.at[r], QY + r, at(dy=r))

    def parts_y(r):
        return send(o_send.at[r], o_recv.at[r], OY + r, at(dy=4 - r))

    def stats_y(r):
        return send(s_send.at[r], s_recv.at[r], SY + r, at(dy=4 - r))

    def attended_z(r):
        return send(a_send.at[r], att.at[z], OZ + r, at(dz=4 - r))

    barrier = pltpu.get_barrier_semaphore()
    partners = [at(dc=1)]
    for r in (1, 2, 3):
        partners += [at(dx=r), at(dy=r), at(dz=r)]
    for device in partners:
        pl.semaphore_signal(barrier, inc=1, device_id=device, device_id_type=MESH)
    pl.semaphore_wait(barrier, len(partners))

    for r in (1, 3, 2):
        queries_z(r).start()
    for r in (1, 3, 2):
        keys_z(r).start()
    qb[0, 0] = q_src[z]
    kv[0, 0, 0] = kv_src[z]
    qs[...] = jnp.zeros_like(qs)
    acc[...] = jnp.zeros_like(acc)
    top[...] = jnp.zeros_like(top)

    def prepare(ry):
        for rz in range(4):
            columns = pl.ds(ry * TILE + rz * ROWS, ROWS)
            scaled = qb[ry, rz].astype(jnp.float32) * (LOG2E * HEAD_DIM**-0.5)
            high = scaled.astype(jnp.bfloat16)
            low = (scaled - high.astype(jnp.float32)).astype(jnp.bfloat16)
            for h in range(2):
                rows = slice(h * HEAD_DIM, (h + 1) * HEAD_DIM)
                qs[h, h * HEAD_DIM : (h + 1) * HEAD_DIM, columns] = high[rows]
                qs[h, ROWS + h * HEAD_DIM : ROWS + (h + 1) * HEAD_DIM, columns] = low[rows]
            q2[:HEAD_DIM, columns] = high[2 * HEAD_DIM :]
            q2[HEAD_DIM:, columns] = low[2 * HEAD_DIM :]

    for r in (1, 3, 2):
        queries_z(r).wait_recv()
    for r in (1, 3, 2):
        queries_y(r).start()
    for r in (1, 3, 2):
        keys_z(r).wait_recv()
    keys_core(0).start()
    for r in (1, 3, 2):
        keys_x(r).start()
    prepare(0)
    keys_core(0).wait_recv()

    def gray(p):
        return p + (p // 2) * (1 - 2 * (p % 2))

    def place(g):
        t, p = g // 4, g % 4
        rx = gray(t)
        ry = gray(p + (t // 3) * (3 - 2 * p))
        return rx, ry

    def score(g, h):
        rx, ry = place(g)
        columns = pl.ds(pl.multiple_of(ry * TILE, TILE), TILE)
        first = 0 if h < 2 else ROWS
        keys = jnp.concatenate(
            [kv[cc, rx, rz, first : first + ROWS, :] for cc in range(2) for rz in range(4)], axis=0
        )
        if h < 2:
            keys = jnp.concatenate([keys, keys], axis=1)
            query = qs[h, :, columns]
        else:
            query = q2[:, columns]
        s = jnp.dot(keys, query, preferred_element_type=jnp.float32)
        sb[h] = s
        old = top[h, :, columns]
        new = jnp.maximum(old, jnp.max(s, axis=0, keepdims=True))
        shrink[h] = jnp.exp2(old - new)
        top[h, :, columns] = new

    def weigh(g, h):
        rx, ry = place(g)
        columns = pl.ds(pl.multiple_of(ry * TILE, TILE), TILE)
        chances = jnp.exp2(sb[h] - top[h, :, columns]).astype(jnp.bfloat16)
        first = KROWS + h * HEAD_DIM
        values = jnp.concatenate(
            [
                jnp.concatenate(
                    [kv[cc, rx, rz, first : first + HEAD_DIM, :], kv[cc, rx, rz, KROWS + GD :, :]],
                    axis=0,
                )
                for cc in range(2)
                for rz in range(4)
            ],
            axis=1,
        )
        acc[h, :, columns] = acc[h, :, columns] * shrink[h] + jnp.dot(
            values, chances, preferred_element_type=jnp.float32
        )

    score(0, 0)

    def step(g, carry):
        for n, r in ((1, 1), (2, 3), (3, 2)):

            @pl.when(g == n - 1)
            def _():
                queries_y(r).wait_recv()
                prepare(r)

        for n, r in ((4, 1), (8, 3), (12, 2)):

            @pl.when(g == n - 1)
            def _():
                keys_x(r).wait_recv()
                keys_core(r).start()
                keys_core(r).wait_recv()

        score(g, 1)
        weigh(g, 0)
        score(g, 2)
        weigh(g, 1)
        score(jnp.minimum(g + 1, 15), 0)
        weigh(g, 2)

        for n, r in ((12, 2), (13, 3), (14, 1), (15, 0)):

            @pl.when(g == n)
            def _():
                columns = pl.ds(r * TILE, TILE)
                o_to, s_to = (o_send, s_send) if r else (o_recv, s_recv)
                for h in range(GH):
                    o_to[r, h * HEAD_DIM : (h + 1) * HEAD_DIM, :] = acc[
                        h, :HEAD_DIM, columns
                    ].astype(jnp.bfloat16)
                    s_to[r, h : h + 1, :] = top[h, :, columns]
                    s_to[r, GH + h : GH + h + 1, :] = acc[h, HEAD_DIM : HEAD_DIM + 1, columns]
                s_to[r, 2 * GH :, :] = jnp.zeros((8 - 2 * GH, TILE), jnp.float32)
                if r:
                    stats_y(r).start()
                    parts_y(r).start()

        return carry

    lax.fori_loop(0, 16, step, 0)

    for r in (2, 3, 1):
        stats_y(r).wait_recv()
        parts_y(r).wait_recv()
    for h in range(GH):
        rows = slice(h * HEAD_DIM, (h + 1) * HEAD_DIM)
        tops = [s_recv[r, h : h + 1, :] for r in range(4)]
        most = jnp.maximum(jnp.maximum(tops[0], tops[1]), jnp.maximum(tops[2], tops[3]))
        total = jnp.exp2(-most)
        weighted = jnp.zeros((HEAD_DIM, TILE), jnp.float32)
        for r in range(4):
            factor = jnp.exp2(tops[r] - most)
            total = total + s_recv[r, GH + h : GH + h + 1, :] * factor
            weighted = weighted + o_recv[r, rows, :].astype(jnp.float32) * factor
        done = (weighted / total).astype(jnp.bfloat16)
        for rz in range(4):
            a_send[rz, rows, :] = done[:, rz * ROWS : (rz + 1) * ROWS]
    for r in (1, 3, 2):
        attended_z(r).start()
    att[z] = a_send[0]
    for r in (1, 3, 2):
        attended_z(r).wait_recv()
    mixed = lax.dot_general(
        att[...].reshape(HEADS * HEAD_DIM, ROWS),
        w_ref[...],
        (((0,), (0,)), ((), ())),
        preferred_element_type=jnp.float32,
    )
    out_ref[...] = mixed.astype(jnp.bfloat16)

    for r in (1, 2, 3):
        for copy in (queries_z, keys_z, queries_y, keys_x, stats_y, parts_y, attended_z):
            copy(r).wait_send()
    for r in range(4):
        keys_core(r).wait_send()


def on_device(queries, keys, values, valid, out_weight):
    flags = (valid > 0).astype(jnp.bfloat16)
    kept = (keys * flags[:, None]).reshape(ROWS, GROUPS, GH, HEAD_DIM)
    first = kept[:, :, :2].reshape(ROWS, GROUPS, ROWS).transpose(1, 0, 2)
    second = jnp.concatenate([kept[:, :, 2], kept[:, :, 2]], axis=-1).transpose(1, 0, 2)
    value_rows = (values * flags[:, None]).T.reshape(GROUPS, GD, ROWS)
    flag_rows = jnp.broadcast_to(
        jnp.concatenate([flags[None, :], jnp.zeros((15, ROWS), jnp.bfloat16)])[None],
        (GROUPS, 16, ROWS),
    )
    kv_src = jnp.concatenate([first, second, value_rows, flag_rows], axis=1)
    q_src = queries.T.reshape(GROUPS, GD, ROWS)
    bf16, f32 = jnp.bfloat16, jnp.float32
    whole = pl.BlockSpec(memory_space=pltpu.VMEM)
    return pl.pallas_call(
        kernel,
        out_shape=jax.ShapeDtypeStruct((ROWS, HEADS * HEAD_DIM), bf16),
        in_specs=[whole] * 3,
        out_specs=whole,
        scratch_shapes=[
            pltpu.VMEM((2, 4, 4, SHARD, ROWS), bf16),
            pltpu.VMEM((4, 4, GD, ROWS), bf16),
            pltpu.VMEM((2, 2 * ROWS, 4 * TILE), bf16),
            pltpu.VMEM((ROWS, 4 * TILE), bf16),
            pltpu.VMEM((GH, 8 * ROWS, TILE), f32),
            pltpu.VMEM((GH, HEAD_DIM + 16, 4 * TILE), f32),
            pltpu.VMEM((GH, 1, 4 * TILE), f32),
            pltpu.VMEM((GH, 1, TILE), f32),
            pltpu.VMEM((4, GD, TILE), bf16),
            pltpu.VMEM((4, 8, TILE), f32),
            pltpu.VMEM((4, GD, TILE), bf16),
            pltpu.VMEM((4, 8, TILE), f32),
            pltpu.VMEM((4, GD, ROWS), bf16),
            pltpu.VMEM((4, GD, ROWS), bf16),
            pltpu.SemaphoreType.DMA((32,)),
            pltpu.SemaphoreType.DMA((32,)),
        ],
        compiler_params=pltpu.CompilerParams(
            collective_id=0, has_side_effects=True, vmem_limit_bytes=56 << 20
        ),
        name="attend",
    )(kv_src, q_src, out_weight)


def solution(mesh):
    return jax.shard_map(
        on_device,
        mesh=mesh,
        in_specs=(
            P(("blk", "inner"), None),
            P(("blk", "inner"), None),
            P(("blk", "inner"), None),
            P(("blk", "inner")),
            P(),
        ),
        out_specs=P(("blk", "inner"), None),
        check_vma=False,
    )
```

time: 534 us -> 79.6 us (0.15)
  waiting for transfers between devices: 195 us -> 0 us
  matrix products: 166 us -> 0 us
  other arithmetic: 77.2 us -> 1.61 us
  Pallas kernels: 0 us -> 72.8 us
  blocking collectives: 52.9 us -> 0 us
  local copies, waits for them, and re-layouts: 25.7 us -> 4.9 us
  between operations: 13.2 us -> 0.08 us
    dot_general x33 -> x0, matrix products: 166 us -> none  [the longest x16 87.4 us: one_block(): jnp.einsum('hqk,khd->hqd', chances, value_heads, preferred_element_type=j...]
    all_gather x3 -> x0, waiting for transfers between devices: 113 us -> none  [the longest x1 57.7 us: on_device(): lax.all_gather(keys, 'inner', axis=0, tiled=True)]
    reduce_scatter x2 -> x0, waiting for transfers between devices: 79.5 us -> none  [the longest x1 48.5 us: combine_loop(): lax.psum_scatter(weighted * shrink[..., None], 'blk', scatter_dimension=1...]
    pallas_call x0 -> x1, Pallas kernels: none -> 72.8 us  [on_device(): pl.pallas_call(kernel, out_shape=jax.ShapeDtypeStruct((ROWS, HEADS * HEAD...]
    reduce_sum x16 -> x0, other arithmetic: 69 us -> none  [one_block(): jnp.sum(chances, axis=-1, dtype=jnp.float32)]
    pmax x1 -> x0, blocking collectives: 26.7 us -> none  [combine_loop(): top = lax.pmax(run_max, 'blk')]
    all_gather x1 -> x0, blocking collectives: 26.2 us -> none  [on_device(): lax.all_gather(flags, 'inner', axis=0, tiled=True)]
    all_gather x3 -> x0, local copies, waits for them, and re-layouts: 11.1 us -> none  [the longest x1 4.75 us: on_device(): lax.all_gather(keys, 'inner', axis=0, tiled=True)]
  transfers between devices with their start and end apart: 5 -> 0, of which waited for: 5 -> 0; matrix products, arithmetic and copies ran while one was open for 3% -> 0% of each run, Pallas kernels for 0% -> 0%
where the time goes in v1:
time: 79.6 us; the launch traced here: 79.4 us
  Pallas kernels  72.8 us (91%)
  local copies, waits for them, and re-layouts  4.9 us (6%)
  other arithmetic  1.61 us (2%)
    pallas_call x1, Pallas kernels, on_device(): pl.pallas_call(kernel, out_shape=jax.ShapeDtypeStruct((ROWS, HEADS * HEAD...  72.8 us
    unnamed x6, local copies, waits for them, and re-layouts  3.93 us

profile of v1, /device:TPU:1, one launch (start us, length us, event | category | flops | bytes accessed | tf_op | source)
XLA Modules:
  0.0 79.4 jit_solution(13667198774539859387)
XLA Ops:
  0.0 0.7 compare_convert_fusion
  0.7 1.1 %copy.11 = bf16[128,768]{0,1:T(8,128)(2,1)S(1)} copy(bf16[128,768]{1,0:T(8,128)(2,1)} %param.7) | data formatting | bytes 393216 | tf_op args[2]
  1.7 1.1 %copy.8 = bf16[128,768]{0,1:T(8,128)(2,1)S(1)} copy(bf16[128,768]{1,0:T(8,128)(2,1)} %param.6) | data formatting | bytes 393216 | tf_op args[1]
  2.9 0.0 copy-start
  2.9 0.1 copy.13
  3.0 0.1 maximum_bitcast_fusion
  3.2 0.1 copy.9
  3.3 0.8 %pad_maximum_fusion.kv_src = bf16[4,464,128]{2,1,0:T(8,128)(2,1)} fusion(bf16[4,16,128]{2,1,0:T(8,128)(2,1)S(1)} %broadcast_in_dim.5, bf16[4,192,128]{2,1,0:T(8,128)(2,1)S(1)} %bitcast.15, bf16[4,128,128]{2,1,0:T(8,128)(2,1)S(1)} %maximum_bitcast_fusion, bf16[4,128,128]{2,1,0:T(8,128)(2,1)S(1)} %bitcast.19), kind=kLoop, calls=%fused_computation | loop fusion | flops 1900544 | bytes 950272 | tf_op jit(solution)/shard_map/concatenate | solution.py:250
  4.2 0.0 copy-done
  4.2 0.8 %copy.12 = bf16[768,128]{1,0:T(8,128)(2,1)} copy(bf16[768,128]{0,1:T(8,128)(2,1)S(1)} %bitcast.20) | data formatting | bytes 393216 | tf_op jit(solution)/shard_map/transpose | solution.py:251
  5.0 72.8 %attend.1 = bf16[128,768]{1,0:T(8,128)(2,1)} custom-call(bf16[4,464,128]{2,1,0:T(8,128)(2,1)} %pad_maximum_fusion.kv_src, bf16[4,192,128]{2,1,0:T(8,128)(2,1)} %bitcast.16, bf16[768,768]{1,0:T(8,128)(2,1)} %w_ref.1), custom_call_target="tpu_custom_call" | custom-call | tf_op jit(solution)/shard_map/attend/pallas_call | solution.py:254
  77.8 1.6 %copy.15 = bf16[128,768]{1,0:T(8,128)(2,1)} copy(bf16[128,768]{1,0:T(8,128)(2,1)} %attend.1) | data formatting | bytes 393216
  (5 shorter events, 0.1 us)
Async XLA Ops:
  2.9 1.3 %copy-start = (bf16[128,768]{1,0:T(8,128)(2,1)S(1)}, bf16[128,768]{1,0:T(8,128)(2,1)}, u32[]{:S(2)}) copy-start(bf16[128,768]{1,0:T(8,128)(2,1)} %param.5) | copy-start | bytes 589828

commit v2 on v1

v2 whole, which is shorter than its diff:
```python
import jax
import jax.numpy as jnp
from jax import lax
from jax.experimental import pallas as pl
from jax.experimental.pallas import tpu as pltpu
from jax.sharding import PartitionSpec as P

HEADS = 12
HEAD_DIM = 64
GROUPS = 4
GH = HEADS // GROUPS
ROWS = 128
GD = GH * HEAD_DIM
TILE = 4 * ROWS
KROWS = ROWS + HEAD_DIM
SHARD = KROWS + GD + 16
PART = GD + 16
LOG2E = 1.4426950408889634
MESH = pl.DeviceIdType.MESH

KA, QA, QY, QZ, KX, KF, KC, KS, OP = 0, 4, 8, 12, 16, 24, 28, 32, 36
COPIES = OP + 16


def kernel(
    q_ref, k_ref, v_ref, valid_ref, out_ref,
    kv_src, q_src, kv, qb, qs, sb, acc, top, shrink, cur, stat, o_send, o_recv,
    send_sem, recv_sem,
):
    bf16, f32 = jnp.bfloat16, jnp.float32
    blk = lax.axis_index("blk")
    inner = lax.axis_index("inner")
    y, x, c = blk % 4, inner // 4, inner % 2
    z = (inner // 2 % 2) * 2 + blk // 4

    def at(dx=0, dy=0, dz=0, dc=0):
        tx, ty, tz, tc = (x + dx) % 4, (y + dy) % 4, (z + dz) % 4, (c + dc) % 2
        return ((tz % 2) * 4 + ty, tx * 4 + (tz // 2) * 2 + tc)

    def send(src, dst, number, device):
        return pltpu.make_async_remote_copy(
            src_ref=src, dst_ref=dst, send_sem=send_sem.at[number], recv_sem=recv_sem.at[number],
            device_id=device, device_id_type=MESH,
        )

    def keys_z(r):
        return send(kv_src.at[(z + r) % 4], kv.at[0, 0, r], KA + r, at(dz=r))

    def queries_z(r):
        return send(q_src.at[(z + r) % 4], qb.at[0, r], QA + r, at(dz=r))

    def queries_y_own(r):
        return send(qb.at[0, 0], qb.at[r, 0], QY + r, at(dy=r))

    def queries_y(r):
        return send(qb.at[0, pl.ds(1, 3)], qb.at[r, pl.ds(1, 3)], QZ + r, at(dy=r))

    def keys_up(rz):
        return send(kv.at[0, 0, rz], kv.at[0, 1, rz], KX + rz, at(dx=1))

    def keys_down(rz):
        return send(kv.at[0, 0, rz], kv.at[0, 3, rz], KX + 4 + rz, at(dx=3))

    def keys_on(rz):
        if rz < 2:
            return send(kv.at[0, 1, rz], kv.at[0, 2, rz], KF + rz, at(dx=1))
        return send(kv.at[0, 3, rz], kv.at[0, 2, rz], KF + rz, at(dx=3))

    def keys_core_own(rz):
        return send(kv.at[0, 0, rz], kv.at[1, 0, rz], KC + rz, at(dc=1))

    def keys_core(rx):
        return send(kv.at[0, rx], kv.at[1, rx], KS + rx, at(dc=1))

    def part(ry, rz):
        return send(
            o_send.at[ry, rz], o_recv.at[ry, rz], OP + 4 * ry + rz, at(dy=4 - ry, dz=4 - rz)
        )

    barrier = pltpu.get_barrier_semaphore()
    partners = [at(dc=1), at(dx=1), at(dx=3)]
    partners += [at(dy=ry, dz=rz) for ry in range(4) for rz in range(4) if ry or rz]
    for device in partners:
        pl.semaphore_signal(barrier, inc=1, device_id=device, device_id_type=MESH)

    turned = q_ref[...].T
    for g in range(GROUPS):
        q_src[g] = turned[g * GD : (g + 1) * GD]
    qb[0, 0] = q_src[z]

    pl.semaphore_wait(barrier, len(partners))
    for r in (1, 3, 2):
        queries_z(r).start()
    for r in (1, 3, 2):
        queries_y_own(r).start()

    flag_row = jnp.where(valid_ref[...] > 0, 1.0, 0.0).astype(f32)
    flag_square = jnp.broadcast_to(flag_row, (ROWS, ROWS))
    key_flags = flag_square.T.astype(bf16)
    value_flags = flag_square[:1].astype(bf16)
    first_row = lax.broadcasted_iota(jnp.int32, (16, ROWS), 0) == 0
    flag_rows = jnp.where(first_row, jnp.broadcast_to(flag_row, (16, ROWS)), 0.0).astype(bf16)
    turned = v_ref[...].T
    for g in range(GROUPS):
        kv_src[g, :ROWS, :] = k_ref[:, g * GD : g * GD + ROWS] * key_flags
        third = k_ref[:, g * GD + ROWS : (g + 1) * GD] * key_flags[:, :HEAD_DIM]
        kv_src[g, ROWS:KROWS, :] = jnp.concatenate([third[:HEAD_DIM], third[HEAD_DIM:]], axis=1)
        kv_src[g, KROWS : KROWS + GD, :] = turned[g * GD : (g + 1) * GD] * value_flags
        kv_src[g, KROWS + GD :, :] = flag_rows
    kv[0, 0, 0] = kv_src[z]
    for r in (1, 3, 2):
        keys_z(r).start()

    def spread(rz):
        keys_up(rz).start()
        keys_down(rz).start()
        keys_core_own(rz).start()

    spread(0)
    qs[...] = jnp.zeros_like(qs)
    acc[...] = jnp.zeros_like(acc)
    top[...] = jnp.zeros_like(top)

    def prepare(ry):
        for rz in range(4):
            columns = pl.ds(ry * TILE + rz * ROWS, ROWS)
            scaled = qb[ry, rz].astype(f32) * (LOG2E * HEAD_DIM**-0.5)
            high = scaled.astype(bf16)
            low = (scaled - high.astype(f32)).astype(bf16)
            for n, h, at_row in ((0, 0, 0), (1, 1, 1), (2, 2, 0), (3, 2, 1)):
                rows = slice(h * HEAD_DIM, (h + 1) * HEAD_DIM)
                qs[n, at_row * HEAD_DIM : (at_row + 1) * HEAD_DIM, columns] = high[rows]
                qs[n, ROWS + at_row * HEAD_DIM : ROWS + (at_row + 1) * HEAD_DIM, columns] = low[
                    rows
                ]

    for r in (1, 3, 2):
        queries_z(r).wait_recv()
    for r in (1, 3, 2):
        queries_y(r).start()
    prepare(0)
    for r in (1, 3, 2):
        keys_z(r).wait_recv()
        spread(r)
    for rz in (0, 1, 3, 2):
        keys_core_own(rz).wait_recv()

    def gray(p):
        return p + (p // 2) * (1 - 2 * (p % 2))

    def place(g):
        if isinstance(g, int) and g < 4:
            return 0, gray(g)
        late = g // 8
        p = (g - 4) * (1 - late) + ((g - 8) // 2) * late
        return 1 + late * (2 - g % 2), gray(p + late * (3 - 2 * p))

    def tile(ry):
        return pl.ds(pl.multiple_of(ry * TILE, TILE), TILE)

    def score(g, h):
        rx, ry = place(g)
        columns = tile(ry)
        rows = slice(0, ROWS) if h < 2 else slice(ROWS, KROWS)
        keys = jnp.concatenate(
            [kv[cc, rx, rz, rows, :] for cc in range(2) for rz in range(4)], axis=0
        )
        keys = jnp.concatenate([keys, keys], axis=1)
        if h < 2:
            s = jnp.dot(keys, qs[h, :, columns], preferred_element_type=f32)
            sb[h] = s.reshape(8, 2, HEAD_DIM, TILE)
            most = jnp.max(s, axis=0, keepdims=True)
        else:
            sa = jnp.dot(keys, qs[2, :, columns], preferred_element_type=f32)
            sb[h, :, 0] = sa.reshape(8, HEAD_DIM, TILE)
            sc = jnp.dot(keys, qs[3, :, columns], preferred_element_type=f32)
            sb[h, :, 1] = sc.reshape(8, HEAD_DIM, TILE)
            most = jnp.maximum(
                jnp.max(sa, axis=0, keepdims=True), jnp.max(sc, axis=0, keepdims=True)
            )
        old = top[h, :, columns]
        new = jnp.maximum(old, most)
        shrink[h] = jnp.exp2(old - new)
        top[h, :, columns] = new
        cur[h] = new

    def weigh(g, h):
        rx, ry = place(g)
        columns = tile(ry)
        chances = jnp.exp2(sb[h].reshape(8 * ROWS, TILE) - cur[h]).astype(bf16)
        first = KROWS + h * HEAD_DIM
        values = jnp.concatenate(
            [
                jnp.concatenate(
                    [kv[cc, rx, rz, first : first + HEAD_DIM, :], kv[cc, rx, rz, KROWS + GD :, :]],
                    axis=0,
                )
                for cc in range(2)
                for rz in range(4)
            ],
            axis=1,
        )
        acc[h, :, columns] = acc[h, :, columns] * shrink[h] + jnp.dot(
            values, chances, preferred_element_type=f32
        )

    def step(g, between=None):
        score(g, 1)
        weigh(g, 0)
        score(g, 2)
        weigh(g, 1)
        if between is not None:
            between()
        if not isinstance(g, int) or g < 15:
            score(g + 1, 0)
        weigh(g, 2)

    def deliver(ry):
        columns = pl.ds(ry * TILE, TILE)
        stat[...] = jnp.zeros_like(stat)
        for h in range(GH):
            left = top[h, :, columns]
            for n in range(3):
                piece = left.astype(bf16).astype(f32)
                stat[n * GH + h : n * GH + h + 1, :] = piece
                left = left - piece
            left = acc[h, HEAD_DIM : HEAD_DIM + 1, columns]
            for n in range(3, 5):
                piece = left.astype(bf16).astype(f32)
                stat[n * GH + h : n * GH + h + 1, :] = piece
                left = left - piece
        for rz in (2, 1, 3, 0):
            to = o_send if ry or rz else o_recv
            columns = pl.ds(ry * TILE + rz * ROWS, ROWS)
            for h in range(GH):
                to[ry, rz, h * HEAD_DIM : (h + 1) * HEAD_DIM, :] = acc[
                    h, :HEAD_DIM, columns
                ].astype(bf16)
            to[ry, rz, GD:, :] = stat[:, rz * ROWS : (rz + 1) * ROWS].astype(bf16)
            if ry or rz:
                part(ry, rz).start()

    def queries_in(ry):
        queries_y_own(ry).wait_recv()
        queries_y(ry).wait_recv()
        prepare(ry)

    score(0, 0)
    step(0, lambda: queries_in(1))
    for rz in (0, 1):
        keys_up(rz).wait_recv()
        keys_on(rz).start()
    keys_down(3).wait_recv()
    keys_on(3).start()
    step(1, lambda: queries_in(3))
    keys_down(2).wait_recv()
    keys_on(2).start()
    for rz in (2, 3):
        keys_up(rz).wait_recv()
    keys_core(1).start()
    for rz in (0, 1):
        keys_down(rz).wait_recv()
    keys_core(3).start()
    step(2, lambda: queries_in(2))
    step(3, lambda: keys_core(1).wait_recv())

    def loop(g, carry):
        @pl.when(g == 5)
        def _():
            for rz in range(4):
                keys_on(rz).wait_recv()
            keys_core(2).start()

        @pl.when(g == 7)
        def _():
            keys_core(3).wait_recv()

        @pl.when(g == 8)
        def _():
            keys_core(2).wait_recv()

        step(g)

        for n, ry in ((9, 2), (11, 3), (13, 1)):

            @pl.when(g == n)
            def _():
                deliver(ry)

        return carry

    lax.fori_loop(4, 15, loop, 0)
    step(15)
    deliver(0)

    for rz in (0, 1, 3, 2):
        for ry in (2, 3, 1, 0):
            if ry or rz:
                part(ry, rz).wait_recv()
        stats = [o_recv[ry, rz, GD:, :].astype(f32) for ry in range(4)]
        for h in range(GH):
            rows = slice(h * HEAD_DIM, (h + 1) * HEAD_DIM)
            row = [[st[n * GH + h : n * GH + h + 1] for n in range(5)] for st in stats]
            tops = [r[0] + r[1] + r[2] for r in row]
            most = jnp.maximum(jnp.maximum(tops[0], tops[1]), jnp.maximum(tops[2], tops[3]))
            total = jnp.exp2(-most)
            weighted = jnp.zeros((HEAD_DIM, ROWS), f32)
            for ry in range(4):
                factor = jnp.exp2(tops[ry] - most)
                total = total + (row[ry][3] + row[ry][4]) * factor
                weighted = weighted + o_recv[ry, rz, rows, :].astype(f32) * factor
            out_ref[(z + rz) % 4, rows, :] = (weighted / total).astype(bf16)

    for r in (1, 2, 3):
        for copy in (queries_z, keys_z, queries_y_own, queries_y, keys_core):
            copy(r).wait_send()
    for r in range(4):
        for copy in (keys_up, keys_down, keys_on, keys_core_own):
            copy(r).wait_send()
        for ry in range(4):
            if ry or r:
                part(ry, r).wait_send()


def on_device(queries, keys, values, valid, out_weight):
    bf16, f32 = jnp.bfloat16, jnp.float32
    whole = pl.BlockSpec(memory_space=pltpu.VMEM)
    attended = pl.pallas_call(
        kernel,
        out_shape=jax.ShapeDtypeStruct((GROUPS, GD, ROWS), bf16),
        in_specs=[whole] * 4,
        out_specs=whole,
        scratch_shapes=[
            pltpu.VMEM((GROUPS, SHARD, ROWS), bf16),
            pltpu.VMEM((GROUPS, GD, ROWS), bf16),
            pltpu.VMEM((2, 4, 4, SHARD, ROWS), bf16),
            pltpu.VMEM((4, 4, GD, ROWS), bf16),
            pltpu.VMEM((4, 2 * ROWS, 4 * TILE), bf16),
            pltpu.VMEM((GH, 8, 2, HEAD_DIM, TILE), f32),
            pltpu.VMEM((GH, HEAD_DIM + 16, 4 * TILE), f32),
            pltpu.VMEM((GH, 1, 4 * TILE), f32),
            pltpu.VMEM((GH, 1, TILE), f32),
            pltpu.VMEM((GH, 1, TILE), f32),
            pltpu.VMEM((16, TILE), f32),
            pltpu.VMEM((4, 4, PART, ROWS), bf16),
            pltpu.VMEM((4, 4, PART, ROWS), bf16),
            pltpu.SemaphoreType.DMA((COPIES,)),
            pltpu.SemaphoreType.DMA((COPIES,)),
        ],
        compiler_params=pltpu.CompilerParams(
            collective_id=0, has_side_effects=True, vmem_limit_bytes=56 << 20
        ),
        name="attend",
    )(queries, keys, values, valid.reshape(1, ROWS))
    mixed = lax.dot_general(
        attended.reshape(HEADS * HEAD_DIM, ROWS),
        out_weight,
        (((0,), (0,)), ((), ())),
        preferred_element_type=f32,
    )
    return mixed.astype(bf16)


def solution(mesh):
    return jax.shard_map(
        on_device,
        mesh=mesh,
        in_specs=(
            P(("blk", "inner"), None),
            P(("blk", "inner"), None),
            P(("blk", "inner"), None),
            P(("blk", "inner")),
            P(),
        ),
        out_specs=P(("blk", "inner"), None),
        check_vma=False,
    )
```

time: 79.6 us -> 56.5 us (0.71)
  Pallas kernels: 72.8 us -> 54.4 us
  local copies, waits for them, and re-layouts: 4.9 us -> 0.01 us
  matrix products: 0 us -> 1.96 us
  other arithmetic: 1.61 us -> 0 us
    pallas_call x1, Pallas kernels: 72.8 us -> 54.4 us  [on_device(): pl.pallas_call(kernel, out_shape=jax.ShapeDtypeStruct((GROUPS, GD, ROWS),...]
    unnamed x6 -> x2, local copies, waits for them, and re-layouts: 3.93 us -> 0.01 us
    dot_general x0 -> x1, matrix products: none -> 1.96 us  [on_device(): lax.dot_general(attended.reshape(HEADS * HEAD_DIM, ROWS), out_weight, (((...]
    transpose x1 -> x0, local copies, waits for them, and re-layouts: 0.81 us -> none  [on_device(): q_src = queries.T.reshape(GROUPS, GD, ROWS)]
    concatenate x1 -> x0, other arithmetic: 0.81 us -> none  [on_device(): kv_src = jnp.concatenate([first, second, value_rows, flag_rows], axis=1)]
where the time goes in v2:
time: 56.5 us; the launch traced here: 56.4 us
  Pallas kernels  54.4 us (96%)
  matrix products  1.96 us (3%)
    pallas_call x1, Pallas kernels, on_device(): pl.pallas_call(kernel, out_shape=jax.ShapeDtypeStruct((GROUPS, GD, ROWS),...  54.4 us
    dot_general x1, matrix products, on_device(): lax.dot_general(attended.reshape(HEADS * HEAD_DIM, ROWS), out_weight, (((...  1.96 us

profile of v2, /device:TPU:1, one launch (start us, length us, event | category | flops | bytes accessed | tf_op | source)
XLA Modules:
  0.0 56.4 jit_solution(7651172533896782562)
XLA Ops:
  0.0 0.0 copy-start
  0.0 54.4 %attend.1 = bf16[4,192,128]{2,1,0:T(8,128)(2,1)} custom-call(bf16[128,768]{1,0:T(8,128)(2,1)} %q_ref.1, bf16[128,768]{1,0:T(8,128)(2,1)} %k_ref.1, bf16[128,768]{1,0:T(8,128)(2,1)} %v_ref.1, s32[1,128]{1,0:T(1,128)} %bitcast.5), custom_call_target="tpu_custom_call" | custom-call | tf_op jit(solution)/shard_map/attend/pallas_call | solution.py:328
  54.4 0.0 copy-done
  54.4 2.0 %convolution_convert_fusion = bf16[128,768]{1,0:T(8,128)(2,1)} fusion(bf16[768,128]{1,0:T(8,128)(2,1)} %bitcast.4, bf16[768,768]{1,0:T(8,128)(2,1)S(1)} %copy-done), kind=kOutput, calls=%fused_computation | convolution fusion | flops 151093248 | bytes 1572864 | tf_op jit(solution)/shard_map/dot_general | solution.py:355
Async XLA Ops:
  0.0 54.4 %copy-start = (bf16[768,768]{1,0:T(8,128)(2,1)S(1)}, bf16[768,768]{1,0:T(8,128)(2,1)}, u32[]{:S(2)}) copy-start(bf16[768,768]{1,0:T(8,128)(2,1)} %param.9) | copy-start | bytes 3538948

commit v3 on v2

v3 whole, which is shorter than its diff:
```python
import jax
import jax.numpy as jnp
from jax import lax
from jax.experimental import pallas as pl
from jax.experimental.pallas import tpu as pltpu
from jax.sharding import PartitionSpec as P

HEADS = 12
HEAD_DIM = 64
GROUPS = 4
GH = HEADS // GROUPS
ROWS = 128
GD = GH * HEAD_DIM
TILE = 4 * ROWS
KROWS = ROWS + HEAD_DIM
SHARD = KROWS + GD + 16
PART = HEAD_DIM + 16
LOG2E = 1.4426950408889634
MESH = pl.DeviceIdType.MESH

KA, QA, QY, QZ, KX, KF, KC, KS, OP, OH = 0, 4, 8, 12, 16, 24, 28, 32, 36, 52
COPIES = OH + 12

KEY_SLOT = {(rx, rz): 4 * rx + rz for rx in range(4) for rz in range(4)}
KEY_SLOT.update({(0, 2): 4, (1, 0): 2, (3, 0): 6, (1, 2): 12})
QUERY_SLOT = {(ry, rz): 4 * ry + rz for ry in range(4) for rz in range(4)}
QUERY_SLOT.update({(0, 2): 4, (1, 0): 2})
TILES = [[owner for owner, n in QUERY_SLOT.items() if n // 4 == t] for t in range(4)]
CHUNK_AT = (0, 0, 0, 0, 1, 1, 1, 1, 3, 3, 2, 2, 3, 2, 3, 2)
TILE_AT = (0, 1, 3, 2, 0, 1, 3, 2, 2, 3, 2, 3, 1, 1, 0, 0)


def lookup(table, g):
    if isinstance(g, int):
        return table[g]
    packed = sum(n << 2 * i for i, n in enumerate(table[4:]))
    return lax.shift_right_logical(jnp.int32(packed), 2 * (g - 4)) % 4


def kernel(
    q_ref, k_ref, v_ref, valid_ref, out_ref,
    kv_src, q_src, kv, qb, qs, sb, acc, top, shrink, cur, stat, o_send, o_recv,
    send_sem, recv_sem,
):
    bf16, f32 = jnp.bfloat16, jnp.float32
    blk = lax.axis_index("blk")
    inner = lax.axis_index("inner")
    y, x, c = blk % 4, inner // 4, inner % 2
    z = (inner // 2 % 2) * 2 + blk // 4

    def at(dx=0, dy=0, dz=0, dc=0):
        tx, ty, tz, tc = (x + dx) % 4, (y + dy) % 4, (z + dz) % 4, (c + dc) % 2
        return ((tz % 2) * 4 + ty, tx * 4 + (tz // 2) * 2 + tc)

    def send(src, dst, number, device):
        return pltpu.make_async_remote_copy(
            src_ref=src, dst_ref=dst, send_sem=send_sem.at[number], recv_sem=recv_sem.at[number],
            device_id=device, device_id_type=MESH,
        )

    def keys(cc, rx, rz):
        return kv.at[cc, KEY_SLOT[rx, rz]]

    def keys_z(r):
        return send(kv_src.at[(z + r) % 4], keys(0, 0, r), KA + r, at(dz=r))

    def queries_z(r):
        return send(q_src.at[(z + r) % 4], qb.at[0, r], QA + r, at(dz=r))

    def queries_y_own(r):
        return send(qb.at[0, 0], qb.at[r, 0], QY + r, at(dy=r))

    def queries_y(r):
        return send(qb.at[0, pl.ds(1, 3)], qb.at[r, pl.ds(1, 3)], QZ + r, at(dy=r))

    def keys_up(rz):
        return send(keys(0, 0, rz), keys(0, 1, rz), KX + rz, at(dx=1))

    def keys_down(rz):
        return send(keys(0, 0, rz), keys(0, 3, rz), KX + 4 + rz, at(dx=3))

    def keys_on(rz):
        if rz < 2:
            return send(keys(0, 1, rz), keys(0, 2, rz), KF + rz, at(dx=1))
        return send(keys(0, 3, rz), keys(0, 2, rz), KF + rz, at(dx=3))

    def keys_core_first(n):
        return send(kv.at[0, n], kv.at[1, n], KC + n, at(dc=1))

    def keys_core(t):
        slots = pl.ds(4 * t, 4)
        return send(kv.at[0, slots], kv.at[1, slots], KS + t, at(dc=1))

    def part(ry, rz):
        device = at(dy=4 - ry, dz=4 - rz)
        return send(o_send.at[ry, rz], o_recv.at[ry, rz], OP + 4 * ry + rz, device)

    def part_head(ry, rz, h):
        device = at(dy=4 - ry, dz=4 - rz)
        number = OH + 4 * h + QUERY_SLOT[ry, rz]
        return send(o_send.at[ry, rz, h], o_recv.at[ry, rz, h], number, device)

    barrier = pltpu.get_barrier_semaphore()
    partners = [at(dc=1), at(dx=1), at(dx=3)]
    partners += [at(dy=ry, dz=rz) for ry in range(4) for rz in range(4) if ry or rz]
    for device in partners:
        pl.semaphore_signal(barrier, inc=1, device_id=device, device_id_type=MESH)

    turned = q_ref[...].T
    for g in range(GROUPS):
        q_src[g] = turned[g * GD : (g + 1) * GD]
    qb[0, 0] = q_src[z]

    pl.semaphore_wait(barrier, len(partners))
    for r in (1, 3, 2):
        queries_z(r).start()
    for r in (1, 3, 2):
        queries_y_own(r).start()

    flag_row = jnp.where(valid_ref[...] > 0, 1.0, 0.0).astype(f32)
    flag_square = jnp.broadcast_to(flag_row, (ROWS, ROWS))
    key_flags = flag_square.T.astype(bf16)
    value_flags = flag_square[:1].astype(bf16)
    first_row = lax.broadcasted_iota(jnp.int32, (16, ROWS), 0) == 0
    flag_rows = jnp.where(first_row, jnp.broadcast_to(flag_row, (16, ROWS)), 0.0).astype(bf16)
    turned = v_ref[...].T
    for g in range(GROUPS):
        kv_src[g, :ROWS, :] = k_ref[:, g * GD : g * GD + ROWS] * key_flags
        third = k_ref[:, g * GD + ROWS : (g + 1) * GD] * key_flags[:, :HEAD_DIM]
        kv_src[g, ROWS:KROWS, :] = jnp.concatenate([third[:HEAD_DIM], third[HEAD_DIM:]], axis=1)
        kv_src[g, KROWS : KROWS + GD, :] = turned[g * GD : (g + 1) * GD] * value_flags
        kv_src[g, KROWS + GD :, :] = flag_rows
    kv[0, KEY_SLOT[0, 0]] = kv_src[z]
    for r in (1, 3):
        keys_z(r).start()
    keys_up(0).start()
    keys_down(0).start()
    keys_core_first(0).start()
    qs[...] = jnp.zeros_like(qs)
    acc[...] = jnp.zeros_like(acc)
    top[...] = jnp.zeros_like(top)
    stat[...] = jnp.zeros_like(stat)

    def prepare(t):
        for ry, rz in TILES[t]:
            columns = pl.ds(QUERY_SLOT[ry, rz] * ROWS, ROWS)
            scaled = qb[ry, rz].astype(f32) * (LOG2E * HEAD_DIM**-0.5)
            high = scaled.astype(bf16)
            low = (scaled - high.astype(f32)).astype(bf16)
            for n, h, at_row in ((0, 0, 0), (1, 1, 1), (2, 2, 0), (3, 2, 1)):
                rows = slice(h * HEAD_DIM, (h + 1) * HEAD_DIM)
                qs[n, at_row * HEAD_DIM : (at_row + 1) * HEAD_DIM, columns] = high[rows]
                qs[n, ROWS + at_row * HEAD_DIM : ROWS + (at_row + 1) * HEAD_DIM, columns] = low[
                    rows
                ]

    for r in (1, 3, 2):
        queries_z(r).wait_recv()
    for r in (1, 3, 2):
        queries_y(r).start()
    queries_y_own(1).wait_recv()
    prepare(0)
    for r in (1, 3):
        keys_z(r).wait_recv()
        keys_core_first(KEY_SLOT[0, r]).start()
        keys_up(r).start()
        keys_down(r).start()
    keys_z(2).start()
    keys_up(0).wait_recv()
    keys_core_first(KEY_SLOT[1, 0]).start()
    keys_on(0).start()
    for n in (0, 1, 3, 2):
        keys_core_first(n).wait_recv()

    def tile(ry):
        return pl.ds(pl.multiple_of(ry * TILE, TILE), TILE)

    def score(g, h):
        chunk = 4 * lookup(CHUNK_AT, g)
        columns = tile(lookup(TILE_AT, g))
        rows = slice(0, ROWS) if h < 2 else slice(ROWS, KROWS)
        keys = jnp.concatenate(
            [kv[cc, chunk + n, rows, :] for cc in range(2) for n in range(4)], axis=0
        )
        keys = jnp.concatenate([keys, keys], axis=1)
        if h < 2:
            s = jnp.dot(keys, qs[h, :, columns], preferred_element_type=f32)
            sb[h] = s.reshape(8, 2, HEAD_DIM, TILE)
            most = jnp.max(s, axis=0, keepdims=True)
        else:
            sa = jnp.dot(keys, qs[2, :, columns], preferred_element_type=f32)
            sb[h, :, 0] = sa.reshape(8, HEAD_DIM, TILE)
            sc = jnp.dot(keys, qs[3, :, columns], preferred_element_type=f32)
            sb[h, :, 1] = sc.reshape(8, HEAD_DIM, TILE)
            most = jnp.maximum(
                jnp.max(sa, axis=0, keepdims=True), jnp.max(sc, axis=0, keepdims=True)
            )
        old = top[h, :, columns]
        new = jnp.maximum(old, most)
        shrink[h] = jnp.exp2(old - new)
        top[h, :, columns] = new
        cur[h] = new

    def weigh(g, h):
        chunk = 4 * lookup(CHUNK_AT, g)
        columns = tile(lookup(TILE_AT, g))
        chances = jnp.exp2(sb[h].reshape(8 * ROWS, TILE) - cur[h]).astype(bf16)
        first = KROWS + h * HEAD_DIM
        values = jnp.concatenate(
            [
                jnp.concatenate(
                    [
                        kv[cc, chunk + n, first : first + HEAD_DIM, :],
                        kv[cc, chunk + n, KROWS + GD :, :],
                    ],
                    axis=0,
                )
                for cc in range(2)
                for n in range(4)
            ],
            axis=1,
        )
        acc[h, :, columns] = acc[h, :, columns] * shrink[h] + jnp.dot(
            values, chances, preferred_element_type=f32
        )

    def step(g, between=None):
        score(g, 1)
        weigh(g, 0)
        score(g, 2)
        weigh(g, 1)
        if between is not None:
            between()
        score(g + 1, 0)
        weigh(g, 2)

    def pack(t, h):
        columns = pl.ds(t * TILE, TILE)
        left = top[h, :, columns]
        for n in range(3):
            piece = left.astype(bf16).astype(f32)
            stat[h, n : n + 1, :] = piece
            left = left - piece
        left = acc[h, HEAD_DIM : HEAD_DIM + 1, columns]
        for n in range(3, 5):
            piece = left.astype(bf16).astype(f32)
            stat[h, n : n + 1, :] = piece
            left = left - piece
        for ry, rz in TILES[t]:
            to = o_send if ry or rz else o_recv
            first = QUERY_SLOT[ry, rz] * ROWS
            to[ry, rz, h, :HEAD_DIM, :] = acc[h, :HEAD_DIM, pl.ds(first, ROWS)].astype(bf16)
            first = first - t * TILE
            to[ry, rz, h, HEAD_DIM:, :] = stat[h, :, first : first + ROWS].astype(bf16)

    def deliver(t):
        for h in range(GH):
            pack(t, h)
        for ry, rz in TILES[t]:
            part(ry, rz).start()

    def deliver_last(h):
        pack(0, h)
        for ry, rz in TILES[0][1:]:
            part_head(ry, rz, h).start()

    def queries_in(ry):
        if ry > 1:
            queries_y_own(ry).wait_recv()
        queries_y(ry).wait_recv()
        prepare(ry)

    score(0, 0)
    step(0, lambda: queries_in(1))
    keys_up(1).wait_recv()
    keys_on(1).start()
    step(1, lambda: queries_in(3))
    keys_z(2).wait_recv()
    keys_up(2).start()
    keys_down(2).start()
    keys_down(3).wait_recv()
    keys_on(3).start()
    keys_up(3).wait_recv()
    keys_down(0).wait_recv()
    keys_core(1).start()
    step(2, lambda: queries_in(2))
    step(3, lambda: keys_core(1).wait_recv())

    def loop(g, carry):
        @pl.when(g == 5)
        def _():
            keys_down(2).wait_recv()
            keys_on(2).start()
            keys_up(2).wait_recv()
            keys_down(1).wait_recv()
            keys_core(3).start()

        @pl.when(g == 7)
        def _():
            keys_core(3).wait_recv()

        @pl.when(g == 8)
        def _():
            for rz in range(4):
                keys_on(rz).wait_recv()
            keys_core(2).start()

        @pl.when(g == 9)
        def _():
            keys_core(2).wait_recv()

        step(g)

        for n, t in ((10, 2), (11, 3), (13, 1)):

            @pl.when(g == n)
            def _():
                deliver(t)

        return carry

    lax.fori_loop(4, 15, loop, 0)
    score(15, 1)
    weigh(15, 0)
    score(15, 2)
    deliver_last(0)
    weigh(15, 1)
    deliver_last(1)
    weigh(15, 2)
    deliver_last(2)

    for t in (2, 3, 1):
        for ry, rz in TILES[t]:
            part(ry, rz).wait_recv()
    for h in range(GH):
        for ry, rz in TILES[0][1:]:
            part_head(ry, rz, h).wait_recv()
        for rz in range(4):
            stats = [o_recv[ry, rz, h, HEAD_DIM:, :].astype(f32) for ry in range(4)]
            row = [[st[n : n + 1] for n in range(5)] for st in stats]
            tops = [r[0] + r[1] + r[2] for r in row]
            most = jnp.maximum(jnp.maximum(tops[0], tops[1]), jnp.maximum(tops[2], tops[3]))
            total = jnp.exp2(-most)
            weighted = jnp.zeros((HEAD_DIM, ROWS), f32)
            for ry in range(4):
                factor = jnp.exp2(tops[ry] - most)
                total = total + (row[ry][3] + row[ry][4]) * factor
                weighted = weighted + o_recv[ry, rz, h, :HEAD_DIM, :].astype(f32) * factor
            rows = slice(h * HEAD_DIM, (h + 1) * HEAD_DIM)
            out_ref[(z + rz) % 4, rows, :] = (weighted / total).astype(bf16)

    for r in (1, 2, 3):
        for copy in (queries_z, keys_z, queries_y_own, queries_y, keys_core):
            copy(r).wait_send()
    for r in range(4):
        for copy in (keys_up, keys_down, keys_on, keys_core_first):
            copy(r).wait_send()
    for t in (1, 2, 3):
        for ry, rz in TILES[t]:
            part(ry, rz).wait_send()
    for h in range(GH):
        for ry, rz in TILES[0][1:]:
            part_head(ry, rz, h).wait_send()


def on_device(queries, keys, values, valid, out_weight):
    bf16, f32 = jnp.bfloat16, jnp.float32
    whole = pl.BlockSpec(memory_space=pltpu.VMEM)
    attended = pl.pallas_call(
        kernel,
        out_shape=jax.ShapeDtypeStruct((GROUPS, GD, ROWS), bf16),
        in_specs=[whole] * 4,
        out_specs=whole,
        scratch_shapes=[
            pltpu.VMEM((GROUPS, SHARD, ROWS), bf16),
            pltpu.VMEM((GROUPS, GD, ROWS), bf16),
            pltpu.VMEM((2, 16, SHARD, ROWS), bf16),
            pltpu.VMEM((4, 4, GD, ROWS), bf16),
            pltpu.VMEM((4, 2 * ROWS, 4 * TILE), bf16),
            pltpu.VMEM((GH, 8, 2, HEAD_DIM, TILE), f32),
            pltpu.VMEM((GH, HEAD_DIM + 16, 4 * TILE), f32),
            pltpu.VMEM((GH, 1, 4 * TILE), f32),
            pltpu.VMEM((GH, 1, TILE), f32),
            pltpu.VMEM((GH, 1, TILE), f32),
            pltpu.VMEM((GH, 16, TILE), f32),
            pltpu.VMEM((4, 4, GH, PART, ROWS), bf16),
            pltpu.VMEM((4, 4, GH, PART, ROWS), bf16),
            pltpu.SemaphoreType.DMA((COPIES,)),
            pltpu.SemaphoreType.DMA((COPIES,)),
        ],
        compiler_params=pltpu.CompilerParams(
            collective_id=0, has_side_effects=True, vmem_limit_bytes=56 << 20
        ),
        name="attend",
    )(queries, keys, values, valid.reshape(1, ROWS))
    mixed = lax.dot_general(
        attended.reshape(HEADS * HEAD_DIM, ROWS),
        out_weight,
        (((0,), (0,)), ((), ())),
        preferred_element_type=f32,
    )
    return mixed.astype(bf16)


def solution(mesh):
    return jax.shard_map(
        on_device,
        mesh=mesh,
        in_specs=(
            P(("blk", "inner"), None),
            P(("blk", "inner"), None),
            P(("blk", "inner"), None),
            P(("blk", "inner")),
            P(),
        ),
        out_specs=P(("blk", "inner"), None),
        check_vma=False,
    )
```

time: 56.5 us -> 59.3 us (1.050)
  Pallas kernels: 54.4 us -> 57.2 us
    pallas_call x1, Pallas kernels: 54.4 us -> 57.2 us  [on_device(): pl.pallas_call(kernel, out_shape=jax.ShapeDtypeStruct((GROUPS, GD, ROWS),...]
where the time goes in v3:
time: 59.3 us; the launch traced here: 59.1 us
  Pallas kernels  57.2 us (96%)
  matrix products  1.96 us (3%)
    pallas_call x1, Pallas kernels, on_device(): pl.pallas_call(kernel, out_shape=jax.ShapeDtypeStruct((GROUPS, GD, ROWS),...  57.2 us
    dot_general x1, matrix products, on_device(): lax.dot_general(attended.reshape(HEADS * HEAD_DIM, ROWS), out_weight, (((...  1.96 us

profile of v3, /device:TPU:1, one launch (start us, length us, event | category | flops | bytes accessed | tf_op | source)
XLA Modules:
  0.0 59.1 jit_solution(15582617305570295871)
XLA Ops:
  0.0 0.0 copy-start
  0.0 57.2 %attend.1 = bf16[4,192,128]{2,1,0:T(8,128)(2,1)} custom-call(bf16[128,768]{1,0:T(8,128)(2,1)} %q_ref.1, bf16[128,768]{1,0:T(8,128)(2,1)} %k_ref.1, bf16[128,768]{1,0:T(8,128)(2,1)} %v_ref.1, s32[1,128]{1,0:T(1,128)} %bitcast.5), custom_call_target="tpu_custom_call" | custom-call | tf_op jit(solution)/shard_map/attend/pallas_call | solution.py:369
  57.2 0.0 copy-done
  57.2 2.0 %convolution_convert_fusion = bf16[128,768]{1,0:T(8,128)(2,1)} fusion(bf16[768,128]{1,0:T(8,128)(2,1)} %bitcast.4, bf16[768,768]{1,0:T(8,128)(2,1)S(1)} %copy-done), kind=kOutput, calls=%fused_computation | convolution fusion | flops 151093248 | bytes 1572864 | tf_op jit(solution)/shard_map/dot_general | solution.py:396
Async XLA Ops:
  0.0 57.2 %copy-start = (bf16[768,768]{1,0:T(8,128)(2,1)S(1)}, bf16[768,768]{1,0:T(8,128)(2,1)}, u32[]{:S(2)}) copy-start(bf16[768,768]{1,0:T(8,128)(2,1)} %param.9) | copy-start | bytes 3538948

commit v4 on v3

--- a/solution.py
+++ b/solution.py
@@ -14,20 +14,30 @@
 TILE = 4 * ROWS
 KROWS = ROWS + HEAD_DIM
 SHARD = KROWS + GD + 16
-PART = HEAD_DIM + 16
+PART = GD + 16
+LAST = HEAD_DIM + 16
 LOG2E = 1.4426950408889634
 MESH = pl.DeviceIdType.MESH
 
-KA, QA, QY, QZ, KX, KF, KC, KS, OP, OH = 0, 4, 8, 12, 16, 24, 28, 32, 36, 52
+KA, QA, QY, KX, KF, KC, OP, OH = 0, 4, 8, 24, 32, 36, 52, 68
 COPIES = OH + 12
 
-KEY_SLOT = {(rx, rz): 4 * rx + rz for rx in range(4) for rz in range(4)}
-KEY_SLOT.update({(0, 2): 4, (1, 0): 2, (3, 0): 6, (1, 2): 12})
-QUERY_SLOT = {(ry, rz): 4 * ry + rz for ry in range(4) for rz in range(4)}
-QUERY_SLOT.update({(0, 2): 4, (1, 0): 2})
-TILES = [[owner for owner, n in QUERY_SLOT.items() if n // 4 == t] for t in range(4)]
-CHUNK_AT = (0, 0, 0, 0, 1, 1, 1, 1, 3, 3, 2, 2, 3, 2, 3, 2)
-TILE_AT = (0, 1, 3, 2, 0, 1, 3, 2, 2, 3, 2, 3, 1, 1, 0, 0)
+CHUNKS = (
+    ((0, 0), (0, 1), (1, 0), (0, 3)),
+    ((3, 0), (1, 1), (3, 1), (0, 2)),
+    ((1, 3), (3, 3), (1, 2), (3, 2)),
+    ((2, 0), (2, 1), (2, 3), (2, 2)),
+)
+KEY_SLOT = {owner: 4 * t + n for t, chunk in enumerate(CHUNKS) for n, owner in enumerate(chunk)}
+TILES = (
+    ((0, 0), (0, 1), (0, 3), (1, 0)),
+    ((0, 2), (1, 1), (3, 0), (2, 0)),
+    ((2, 1), (2, 3), (2, 2), (3, 2)),
+    ((3, 1), (1, 3), (3, 3), (1, 2)),
+)
+QUERY_SLOT = {owner: 4 * t + n for t, tile in enumerate(TILES) for n, owner in enumerate(tile)}
+CHUNK_AT = (0, 0, 0, 0, 1, 1, 1, 2, 2, 2, 3, 3, 3, 1, 2, 3)
+TILE_AT = (0, 1, 3, 2, 2, 3, 1, 2, 3, 1, 2, 3, 1, 0, 0, 0)
 
 
 def lookup(table, g):
@@ -39,7 +49,7 @@
 
 def kernel(
     q_ref, k_ref, v_ref, valid_ref, out_ref,
-    kv_src, q_src, kv, qb, qs, sb, acc, top, shrink, cur, stat, o_send, o_recv,
+    kv_src, q_src, kv, qb, qs, sb, acc, top, shrink, cur, stat, stat_last, o_send, o_recv, h_send, h_recv,
     send_sem, recv_sem,
 ):
     bf16, f32 = jnp.bfloat16, jnp.float32
@@ -67,11 +77,8 @@
     def queries_z(r):
         return send(q_src.at[(z + r) % 4], qb.at[0, r], QA + r, at(dz=r))
 
-    def queries_y_own(r):
-        return send(qb.at[0, 0], qb.at[r, 0], QY + r, at(dy=r))
-
-    def queries_y(r):
-        return send(qb.at[0, pl.ds(1, 3)], qb.at[r, pl.ds(1, 3)], QZ + r, at(dy=r))
+    def queries_y(ry, rz):
+        return send(qb.at[0, rz], qb.at[ry, rz], QY + 4 * ry + rz, at(dy=ry))
 
     def keys_up(rz):
         return send(keys(0, 0, rz), keys(0, 1, rz), KX + rz, at(dx=1))
@@ -80,25 +87,20 @@
         return send(keys(0, 0, rz), keys(0, 3, rz), KX + 4 + rz, at(dx=3))
 
     def keys_on(rz):
-        if rz < 2:
+        if rz in (0, 3):
             return send(keys(0, 1, rz), keys(0, 2, rz), KF + rz, at(dx=1))
         return send(keys(0, 3, rz), keys(0, 2, rz), KF + rz, at(dx=3))
 
-    def keys_core_first(n):
-        return send(kv.at[0, n], kv.at[1, n], KC + n, at(dc=1))
-
-    def keys_core(t):
-        slots = pl.ds(4 * t, 4)
-        return send(kv.at[0, slots], kv.at[1, slots], KS + t, at(dc=1))
+    def keys_core(rx, rz):
+        return send(keys(0, rx, rz), keys(1, rx, rz), KC + KEY_SLOT[rx, rz], at(dc=1))
 
     def part(ry, rz):
-        device = at(dy=4 - ry, dz=4 - rz)
-        return send(o_send.at[ry, rz], o_recv.at[ry, rz], OP + 4 * ry + rz, device)
+        n = QUERY_SLOT[ry, rz]
+        return send(o_send.at[n], o_recv.at[n], OP + n, at(dy=4 - ry, dz=4 - rz))
 
     def part_head(ry, rz, h):
-        device = at(dy=4 - ry, dz=4 - rz)
-        number = OH + 4 * h + QUERY_SLOT[ry, rz]
-        return send(o_send.at[ry, rz, h], o_recv.at[ry, rz, h], number, device)
+        n = QUERY_SLOT[ry, rz]
+        return send(h_send.at[n, h], h_recv.at[n, h], OH + 4 * h + n, at(dy=4 - ry, dz=4 - rz))
 
     barrier = pltpu.get_barrier_semaphore()
     partners = [at(dc=1), at(dx=1), at(dx=3)]
@@ -115,7 +117,7 @@
     for r in (1, 3, 2):
         queries_z(r).start()
     for r in (1, 3, 2):
-        queries_y_own(r).start()
+        queries_y(r, 0).start()
 
     flag_row = jnp.where(valid_ref[...] > 0, 1.0, 0.0).astype(f32)
     flag_square = jnp.broadcast_to(flag_row, (ROWS, ROWS))
@@ -135,11 +137,12 @@
         keys_z(r).start()
     keys_up(0).start()
     keys_down(0).start()
-    keys_core_first(0).start()
+    keys_core(0, 0).start()
     qs[...] = jnp.zeros_like(qs)
     acc[...] = jnp.zeros_like(acc)
     top[...] = jnp.zeros_like(top)
     stat[...] = jnp.zeros_like(stat)
+    stat_last[...] = jnp.zeros_like(stat_last)
 
     def prepare(t):
         for ry, rz in TILES[t]:
@@ -156,21 +159,30 @@
 
     for r in (1, 3, 2):
         queries_z(r).wait_recv()
+        queries_y(1, r).start()
+        queries_y(3, r).start()
+    queries_y(1, 0).wait_recv()
+    prepare(0)
     for r in (1, 3, 2):
-        queries_y(r).start()
-    queries_y_own(1).wait_recv()
-    prepare(0)
+        queries_y(2, r).start()
+
+    def keys_in(copy, rx, rz):
+        copy(rz).wait_recv()
+        keys_core(rx, rz).start()
+
+    def chunk_in(t):
+        for rx, rz in CHUNKS[t]:
+            keys_core(rx, rz).wait_recv()
+
     for r in (1, 3):
-        keys_z(r).wait_recv()
-        keys_core_first(KEY_SLOT[0, r]).start()
+        keys_in(keys_z, 0, r)
         keys_up(r).start()
         keys_down(r).start()
     keys_z(2).start()
-    keys_up(0).wait_recv()
-    keys_core_first(KEY_SLOT[1, 0]).start()
+    keys_in(keys_up, 1, 0)
     keys_on(0).start()
-    for n in (0, 1, 3, 2):
-        keys_core_first(n).wait_recv()
+    keys_in(keys_down, 3, 0)
+    chunk_in(0)
 
     def tile(ry):
         return pl.ds(pl.multiple_of(ry * TILE, TILE), TILE)
@@ -234,84 +246,86 @@
         score(g + 1, 0)
         weigh(g, 2)
 
-    def pack(t, h):
+    def pieces(store, at_row, value, n):
+        for i in range(n):
+            piece = value.astype(bf16).astype(f32)
+            store[at_row(i), :] = piece
+            value = value - piece
+
+    def deliver(t):
         columns = pl.ds(t * TILE, TILE)
-        left = top[h, :, columns]
-        for n in range(3):
-            piece = left.astype(bf16).astype(f32)
-            stat[h, n : n + 1, :] = piece
-            left = left - piece
-        left = acc[h, HEAD_DIM : HEAD_DIM + 1, columns]
-        for n in range(3, 5):
-            piece = left.astype(bf16).astype(f32)
-            stat[h, n : n + 1, :] = piece
-            left = left - piece
+        for h in range(GH):
+            pieces(stat, lambda i: pl.ds(GH * i + h, 1), top[h, :, columns], 3)
+            total = acc[h, HEAD_DIM : HEAD_DIM + 1, columns]
+            pieces(stat, lambda i: pl.ds(GH * (i + 3) + h, 1), total, 2)
+        for n, (ry, rz) in enumerate(TILES[t]):
+            slot = 4 * t + n
+            for h in range(GH):
+                rows = pl.ds(h * HEAD_DIM, HEAD_DIM)
+                o_send[slot, rows, :] = acc[h, :HEAD_DIM, pl.ds(slot * ROWS, ROWS)].astype(bf16)
+            o_send[slot, GD:, :] = stat[:, n * ROWS : (n + 1) * ROWS].astype(bf16)
+            part(ry, rz).start()
+
+    def deliver_last(h):
+        columns = pl.ds(0, TILE)
+        store = stat_last.at[h]
+        pieces(store, lambda i: pl.ds(i, 1), top[h, :, columns], 3)
+        pieces(store, lambda i: pl.ds(i + 3, 1), acc[h, HEAD_DIM : HEAD_DIM + 1, columns], 2)
+        for n in (1, 2, 3, 0):
+            to = h_send if n else h_recv
+            to[n, h, :HEAD_DIM, :] = acc[h, :HEAD_DIM, pl.ds(n * ROWS, ROWS)].astype(bf16)
+            to[n, h, HEAD_DIM:, :] = stat_last[h, :, n * ROWS : (n + 1) * ROWS].astype(bf16)
+            if n:
+                part_head(*TILES[0][n], h).start()
+
+    def queries_in(t):
         for ry, rz in TILES[t]:
-            to = o_send if ry or rz else o_recv
-            first = QUERY_SLOT[ry, rz] * ROWS
-            to[ry, rz, h, :HEAD_DIM, :] = acc[h, :HEAD_DIM, pl.ds(first, ROWS)].astype(bf16)
-            first = first - t * TILE
-            to[ry, rz, h, HEAD_DIM:, :] = stat[h, :, first : first + ROWS].astype(bf16)
-
-    def deliver(t):
-        for h in range(GH):
-            pack(t, h)
-        for ry, rz in TILES[t]:
-            part(ry, rz).start()
-
-    def deliver_last(h):
-        pack(0, h)
-        for ry, rz in TILES[0][1:]:
-            part_head(ry, rz, h).start()
-
-    def queries_in(ry):
-        if ry > 1:
-            queries_y_own(ry).wait_recv()
-        queries_y(ry).wait_recv()
-        prepare(ry)
+            if ry:
+                queries_y(ry, rz).wait_recv()
+        prepare(t)
 
     score(0, 0)
     step(0, lambda: queries_in(1))
-    keys_up(1).wait_recv()
-    keys_on(1).start()
-    step(1, lambda: queries_in(3))
-    keys_z(2).wait_recv()
+    keys_in(keys_z, 0, 2)
     keys_up(2).start()
     keys_down(2).start()
-    keys_down(3).wait_recv()
+    step(1, lambda: queries_in(3))
+    keys_in(keys_down, 3, 1)
+    keys_on(1).start()
+    keys_in(keys_up, 1, 1)
+    step(2, lambda: queries_in(2))
+    keys_in(keys_up, 1, 3)
     keys_on(3).start()
-    keys_up(3).wait_recv()
-    keys_down(0).wait_recv()
-    keys_core(1).start()
-    step(2, lambda: queries_in(2))
-    step(3, lambda: keys_core(1).wait_recv())
+    keys_in(keys_down, 3, 3)
+    step(3, lambda: chunk_in(1))
 
     def loop(g, carry):
+        @pl.when(g == 4)
+        def _():
+            keys_in(keys_down, 3, 2)
+            keys_on(2).start()
+            keys_in(keys_up, 1, 2)
+
         @pl.when(g == 5)
         def _():
-            keys_down(2).wait_recv()
-            keys_on(2).start()
-            keys_up(2).wait_recv()
-            keys_down(1).wait_recv()
-            keys_core(3).start()
-
-        @pl.when(g == 7)
-        def _():
-            keys_core(3).wait_recv()
+            keys_in(keys_on, 2, 0)
+            keys_in(keys_on, 2, 1)
 
         @pl.when(g == 8)
         def _():
-            for rz in range(4):
-                keys_on(rz).wait_recv()
-            keys_core(2).start()
-
-        @pl.when(g == 9)
-        def _():
-            keys_core(2).wait_recv()
-
-        step(g)
-
-        for n, t in ((10, 2), (11, 3), (13, 1)):
+            keys_in(keys_on, 2, 3)
+            keys_in(keys_on, 2, 2)
+
+        def between():
+            for n, t in ((6, 2), (9, 3)):
+
+                @pl.when(g == n)
+                def _():
+                    chunk_in(t)
+
+        step(g, between)
+
+        for n, t in ((10, 2), (11, 3), (12, 1)):
 
             @pl.when(g == n)
             def _():
@@ -336,8 +350,17 @@
         for ry, rz in TILES[0][1:]:
             part_head(ry, rz, h).wait_recv()
         for rz in range(4):
-            stats = [o_recv[ry, rz, h, HEAD_DIM:, :].astype(f32) for ry in range(4)]
-            row = [[st[n : n + 1] for n in range(5)] for st in stats]
+            row, weights = [], []
+            for ry in range(4):
+                n = QUERY_SLOT[ry, rz]
+                if n < 4:
+                    stats = h_recv[n, h, HEAD_DIM:, :].astype(f32)
+                    row.append([stats[i : i + 1] for i in range(5)])
+                    weights.append(h_recv[n, h, :HEAD_DIM, :])
+                else:
+                    stats = o_recv[n, GD:, :].astype(f32)
+                    row.append([stats[GH * i + h : GH * i + h + 1] for i in range(5)])
+                    weights.append(o_recv[n, h * HEAD_DIM : (h + 1) * HEAD_DIM, :])
             tops = [r[0] + r[1] + r[2] for r in row]
             most = jnp.maximum(jnp.maximum(tops[0], tops[1]), jnp.maximum(tops[2], tops[3]))
             total = jnp.exp2(-most)
@@ -345,16 +368,20 @@
             for ry in range(4):
                 factor = jnp.exp2(tops[ry] - most)
                 total = total + (row[ry][3] + row[ry][4]) * factor
-                weighted = weighted + o_recv[ry, rz, h, :HEAD_DIM, :].astype(f32) * factor
+                weighted = weighted + weights[ry].astype(f32) * factor
             rows = slice(h * HEAD_DIM, (h + 1) * HEAD_DIM)
             out_ref[(z + rz) % 4, rows, :] = (weighted / total).astype(bf16)
 
     for r in (1, 2, 3):
-        for copy in (queries_z, keys_z, queries_y_own, queries_y, keys_core):
+        for copy in (queries_z, keys_z):
             copy(r).wait_send()
     for r in range(4):
-        for copy in (keys_up, keys_down, keys_on, keys_core_first):
+        for copy in (keys_up, keys_down, keys_on):
             copy(r).wait_send()
+        for rx in range(4):
+            keys_core(rx, r).wait_send()
+        for ry in (1, 2, 3):
+            queries_y(ry, r).wait_send()
     for t in (1, 2, 3):
         for ry, rz in TILES[t]:
             part(ry, rz).wait_send()
@@ -382,9 +409,12 @@
             pltpu.VMEM((GH, 1, 4 * TILE), f32),
             pltpu.VMEM((GH, 1, TILE), f32),
             pltpu.VMEM((GH, 1, TILE), f32),
+            pltpu.VMEM((16, TILE), f32),
             pltpu.VMEM((GH, 16, TILE), f32),
-            pltpu.VMEM((4, 4, GH, PART, ROWS), bf16),
-            pltpu.VMEM((4, 4, GH, PART, ROWS), bf16),
+            pltpu.VMEM((16, PART, ROWS), bf16),
+            pltpu.VMEM((16, PART, ROWS), bf16),
+            pltpu.VMEM((4, GH, LAST, ROWS), bf16),
+            pltpu.VMEM((4, GH, LAST, ROWS), bf16),
             pltpu.SemaphoreType.DMA((COPIES,)),
             pltpu.SemaphoreType.DMA((COPIES,)),
         ],

time: 59.3 us -> 55.3 us (0.933)
  Pallas kernels: 57.2 us -> 52.6 us
    pallas_call x1, Pallas kernels: 57.2 us -> 52.6 us  [on_device(): pl.pallas_call(kernel, out_shape=jax.ShapeDtypeStruct((GROUPS, GD, ROWS),...]
where the time goes in v4:
time: 55.3 us; the launch traced here: 54.6 us
  Pallas kernels  52.6 us (95%)
  matrix products  1.96 us (4%)
    pallas_call x1, Pallas kernels, on_device(): pl.pallas_call(kernel, out_shape=jax.ShapeDtypeStruct((GROUPS, GD, ROWS),...  52.6 us
    dot_general x1, matrix products, on_device(): lax.dot_general(attended.reshape(HEADS * HEAD_DIM, ROWS), out_weight, (((...  1.96 us

profile of v4, /device:TPU:1, one launch (start us, length us, event | category | flops | bytes accessed | tf_op | source)
XLA Modules:
  0.0 54.6 jit_solution(8706863451874248763)
XLA Ops:
  0.0 0.0 copy-start
  0.0 52.6 %attend.1 = bf16[4,192,128]{2,1,0:T(8,128)(2,1)} custom-call(bf16[128,768]{1,0:T(8,128)(2,1)} %q_ref.1, bf16[128,768]{1,0:T(8,128)(2,1)} %k_ref.1, bf16[128,768]{1,0:T(8,128)(2,1)} %v_ref.1, s32[1,128]{1,0:T(1,128)} %bitcast.5), custom_call_target="tpu_custom_call" | custom-call | tf_op jit(solution)/shard_map/attend/pallas_call | solution.py:396
  52.6 0.0 copy-done
  52.6 2.0 %convolution_convert_fusion = bf16[128,768]{1,0:T(8,128)(2,1)} fusion(bf16[768,128]{1,0:T(8,128)(2,1)} %bitcast.4, bf16[768,768]{1,0:T(8,128)(2,1)S(1)} %copy-done), kind=kOutput, calls=%fused_computation | convolution fusion | flops 151093248 | bytes 1572864 | tf_op jit(solution)/shard_map/dot_general | solution.py:426
Async XLA Ops:
  0.0 52.6 %copy-start = (bf16[768,768]{1,0:T(8,128)(2,1)S(1)}, bf16[768,768]{1,0:T(8,128)(2,1)}, u32[]{:S(2)}) copy-start(bf16[768,768]{1,0:T(8,128)(2,1)} %param.9) | copy-start | bytes 3538948

commit v5 on v4

--- a/solution.py
+++ b/solution.py
@@ -36,8 +36,8 @@
     ((3, 1), (1, 3), (3, 3), (1, 2)),
 )
 QUERY_SLOT = {owner: 4 * t + n for t, tile in enumerate(TILES) for n, owner in enumerate(tile)}
-CHUNK_AT = (0, 0, 0, 0, 1, 1, 1, 2, 2, 2, 3, 3, 3, 1, 2, 3)
-TILE_AT = (0, 1, 3, 2, 2, 3, 1, 2, 3, 1, 2, 3, 1, 0, 0, 0)
+CHUNK_AT = (0, 0, 0, 1, 1, 0, 1, 2, 2, 2, 3, 3, 3, 1, 2, 3)
+TILE_AT = (0, 1, 3, 3, 1, 2, 2, 2, 3, 1, 2, 3, 1, 0, 0, 0)
 
 
 def lookup(table, g):
@@ -286,44 +286,45 @@
 
     score(0, 0)
     step(0, lambda: queries_in(1))
+    step(1, lambda: queries_in(3))
     keys_in(keys_z, 0, 2)
+    keys_in(keys_down, 3, 1)
+    keys_in(keys_up, 1, 1)
     keys_up(2).start()
     keys_down(2).start()
-    step(1, lambda: queries_in(3))
-    keys_in(keys_down, 3, 1)
     keys_on(1).start()
-    keys_in(keys_up, 1, 1)
-    step(2, lambda: queries_in(2))
+    step(2, lambda: chunk_in(1))
+    step(3)
     keys_in(keys_up, 1, 3)
     keys_on(3).start()
     keys_in(keys_down, 3, 3)
-    step(3, lambda: chunk_in(1))
+    step(4, lambda: queries_in(2))
 
     def loop(g, carry):
-        @pl.when(g == 4)
+        @pl.when(g == 5)
         def _():
             keys_in(keys_down, 3, 2)
             keys_on(2).start()
             keys_in(keys_up, 1, 2)
 
-        @pl.when(g == 5)
+        @pl.when(g == 6)
         def _():
-            keys_in(keys_on, 2, 0)
-            keys_in(keys_on, 2, 1)
+            chunk_in(2)
+
+        @pl.when(g == 7)
+        def _():
+            for rz in (0, 1, 3):
+                keys_in(keys_on, 2, rz)
 
         @pl.when(g == 8)
         def _():
-            keys_in(keys_on, 2, 3)
             keys_in(keys_on, 2, 2)
 
-        def between():
-            for n, t in ((6, 2), (9, 3)):
-
-                @pl.when(g == n)
-                def _():
-                    chunk_in(t)
-
-        step(g, between)
+        @pl.when(g == 9)
+        def _():
+            chunk_in(3)
+
+        step(g)
 
         for n, t in ((10, 2), (11, 3), (12, 1)):
 
@@ -333,7 +334,7 @@
 
         return carry
 
-    lax.fori_loop(4, 15, loop, 0)
+    lax.fori_loop(5, 15, loop, 0)
     score(15, 1)
     weigh(15, 0)
     score(15, 2)

time: 55.3 us -> 55 us (level)
  no operation moved by 1% of the time
where the time goes in v5:
time: 55 us; the launch traced here: 54.8 us
  Pallas kernels  52.8 us (96%)
  matrix products  1.96 us (4%)
    pallas_call x1, Pallas kernels, on_device(): pl.pallas_call(kernel, out_shape=jax.ShapeDtypeStruct((GROUPS, GD, ROWS),...  52.8 us
    dot_general x1, matrix products, on_device(): lax.dot_general(attended.reshape(HEADS * HEAD_DIM, ROWS), out_weight, (((...  1.96 us

profile of v5, /device:TPU:1, one launch (start us, length us, event | category | flops | bytes accessed | tf_op | source)
XLA Modules:
  0.0 54.8 jit_solution(1121956307080375911)
XLA Ops:
  0.0 0.0 copy-start
  0.0 52.8 %attend.1 = bf16[4,192,128]{2,1,0:T(8,128)(2,1)} custom-call(bf16[128,768]{1,0:T(8,128)(2,1)} %q_ref.1, bf16[128,768]{1,0:T(8,128)(2,1)} %k_ref.1, bf16[128,768]{1,0:T(8,128)(2,1)} %v_ref.1, s32[1,128]{1,0:T(1,128)} %bitcast.5), custom_call_target="tpu_custom_call" | custom-call | tf_op jit(solution)/shard_map/attend/pallas_call | solution.py:397
  52.8 0.0 copy-done
  52.9 2.0 %convolution_convert_fusion = bf16[128,768]{1,0:T(8,128)(2,1)} fusion(bf16[768,128]{1,0:T(8,128)(2,1)} %bitcast.4, bf16[768,768]{1,0:T(8,128)(2,1)S(1)} %copy-done), kind=kOutput, calls=%fused_computation | convolution fusion | flops 151093248 | bytes 1572864 | tf_op jit(solution)/shard_map/dot_general | solution.py:427
Async XLA Ops:
  0.0 52.8 %copy-start = (bf16[768,768]{1,0:T(8,128)(2,1)S(1)}, bf16[768,768]{1,0:T(8,128)(2,1)}, u32[]{:S(2)}) copy-start(bf16[768,768]{1,0:T(8,128)(2,1)} %param.9) | copy-start | bytes 3538948

commit v6 on v5

--- a/solution.py
+++ b/solution.py
@@ -36,8 +36,8 @@
     ((3, 1), (1, 3), (3, 3), (1, 2)),
 )
 QUERY_SLOT = {owner: 4 * t + n for t, tile in enumerate(TILES) for n, owner in enumerate(tile)}
-CHUNK_AT = (0, 0, 0, 1, 1, 0, 1, 2, 2, 2, 3, 3, 3, 1, 2, 3)
-TILE_AT = (0, 1, 3, 3, 1, 2, 2, 2, 3, 1, 2, 3, 1, 0, 0, 0)
+CHUNK_AT = (0, 0, 0, 1, 1, 0, 1, 2, 2, 3, 3, 2, 3, 1, 2, 3)
+TILE_AT = (0, 1, 3, 3, 1, 2, 2, 2, 3, 2, 3, 1, 1, 0, 0, 0)
 
 
 def lookup(table, g):
@@ -313,20 +313,16 @@
 
         @pl.when(g == 7)
         def _():
-            for rz in (0, 1, 3):
+            for rz in (0, 1, 3, 2):
                 keys_in(keys_on, 2, rz)
 
         @pl.when(g == 8)
         def _():
-            keys_in(keys_on, 2, 2)
-
-        @pl.when(g == 9)
-        def _():
             chunk_in(3)
 
         step(g)
 
-        for n, t in ((10, 2), (11, 3), (12, 1)):
+        for n, t in ((9, 2), (10, 3), (12, 1)):
 
             @pl.when(g == n)
             def _():

time: 55 us -> 53.4 us (0.971)
  Pallas kernels: 52.8 us -> 51.3 us
    pallas_call x1, Pallas kernels: 52.8 us -> 51.3 us  [on_device(): pl.pallas_call(kernel, out_shape=jax.ShapeDtypeStruct((GROUPS, GD, ROWS),...]
where the time goes in v6:
time: 53.4 us; the launch traced here: 53.3 us
  Pallas kernels  51.3 us (96%)
  matrix products  1.96 us (4%)
    pallas_call x1, Pallas kernels, on_device(): pl.pallas_call(kernel, out_shape=jax.ShapeDtypeStruct((GROUPS, GD, ROWS),...  51.3 us
    dot_general x1, matrix products, on_device(): lax.dot_general(attended.reshape(HEADS * HEAD_DIM, ROWS), out_weight, (((...  1.96 us

profile of v6, /device:TPU:1, one launch (start us, length us, event | category | flops | bytes accessed | tf_op | source)
XLA Modules:
  0.0 53.3 jit_solution(6146013847152890886)
XLA Ops:
  0.0 0.0 copy-start
  0.0 51.3 %attend.1 = bf16[4,192,128]{2,1,0:T(8,128)(2,1)} custom-call(bf16[128,768]{1,0:T(8,128)(2,1)} %q_ref.1, bf16[128,768]{1,0:T(8,128)(2,1)} %k_ref.1, bf16[128,768]{1,0:T(8,128)(2,1)} %v_ref.1, s32[1,128]{1,0:T(1,128)} %bitcast.5), custom_call_target="tpu_custom_call" | custom-call | tf_op jit(solution)/shard_map/attend/pallas_call | solution.py:393
  51.3 0.0 copy-done
  51.3 2.0 %convolution_convert_fusion = bf16[128,768]{1,0:T(8,128)(2,1)} fusion(bf16[768,128]{1,0:T(8,128)(2,1)} %bitcast.4, bf16[768,768]{1,0:T(8,128)(2,1)S(1)} %copy-done), kind=kOutput, calls=%fused_computation | convolution fusion | flops 151093248 | bytes 1572864 | tf_op jit(solution)/shard_map/dot_general | solution.py:423
Async XLA Ops:
  0.0 51.3 %copy-start = (bf16[768,768]{1,0:T(8,128)(2,1)S(1)}, bf16[768,768]{1,0:T(8,128)(2,1)}, u32[]{:S(2)}) copy-start(bf16[768,768]{1,0:T(8,128)(2,1)} %param.9) | copy-start | bytes 3538948

commit v7 on v6

--- a/solution.py
+++ b/solution.py
@@ -306,6 +306,8 @@
             keys_in(keys_down, 3, 2)
             keys_on(2).start()
             keys_in(keys_up, 1, 2)
+            for rz in (0, 1):
+                keys_in(keys_on, 2, rz)
 
         @pl.when(g == 6)
         def _():
@@ -313,7 +315,7 @@
 
         @pl.when(g == 7)
         def _():
-            for rz in (0, 1, 3, 2):
+            for rz in (3, 2):
                 keys_in(keys_on, 2, rz)
 
         @pl.when(g == 8)

time: 53.4 us -> 53.4 us (level)
  no operation moved by 1% of the time
where the time goes in v7:
time: 53.4 us; the launch traced here: 53.3 us
  Pallas kernels  51.3 us (96%)
  matrix products  1.96 us (4%)
    pallas_call x1, Pallas kernels, on_device(): pl.pallas_call(kernel, out_shape=jax.ShapeDtypeStruct((GROUPS, GD, ROWS),...  51.3 us
    dot_general x1, matrix products, on_device(): lax.dot_general(attended.reshape(HEADS * HEAD_DIM, ROWS), out_weight, (((...  1.96 us

profile of v7, /device:TPU:1, one launch (start us, length us, event | category | flops | bytes accessed | tf_op | source)
XLA Modules:
  0.0 53.3 jit_solution(17843311983332823644)
XLA Ops:
  0.0 0.0 copy-start
  0.0 51.3 %attend.1 = bf16[4,192,128]{2,1,0:T(8,128)(2,1)} custom-call(bf16[128,768]{1,0:T(8,128)(2,1)} %q_ref.1, bf16[128,768]{1,0:T(8,128)(2,1)} %k_ref.1, bf16[128,768]{1,0:T(8,128)(2,1)} %v_ref.1, s32[1,128]{1,0:T(1,128)} %bitcast.5), custom_call_target="tpu_custom_call" | custom-call | tf_op jit(solution)/shard_map/attend/pallas_call | solution.py:395
  51.3 0.0 copy-done
  51.3 2.0 %convolution_convert_fusion = bf16[128,768]{1,0:T(8,128)(2,1)} fusion(bf16[768,128]{1,0:T(8,128)(2,1)} %bitcast.4, bf16[768,768]{1,0:T(8,128)(2,1)S(1)} %copy-done), kind=kOutput, calls=%fused_computation | convolution fusion | flops 151093248 | bytes 1572864 | tf_op jit(solution)/shard_map/dot_general | solution.py:425
Async XLA Ops:
  0.0 51.3 %copy-start = (bf16[768,768]{1,0:T(8,128)(2,1)S(1)}, bf16[768,768]{1,0:T(8,128)(2,1)}, u32[]{:S(2)}) copy-start(bf16[768,768]{1,0:T(8,128)(2,1)} %param.9) | copy-start | bytes 3538948
